TPU v7x, 32 devices: a whole 2x2x4 slice. The times are simulated.
32 devices in a mesh: rep: 2 (over core), grp: 16 (over z, y, x).
Axes of the slice: x: 2, y: 2, z: 4, core: 2. Of those that a mesh axis runs over, the one named last changes fastest.
Arguments:
- grad_parts: float32 [2, 1024, 9216], P('rep', 'grp'), may hold values from -6 to 6
- gain_grad_parts: float32 [2, 2, 1024], P('rep', None, 'grp'), may hold values from -6 to 6
- weights: float32 [1024, 9216], P('grp'), may hold values from -0.1875 to 0.1875
- basis: float32 [1024, 256], P('grp'), may hold values from -0.1875 to 0.1875
- moment_first: float32 [9216, 256], P('grp'), may hold values from -12 to 12
- moment_second: float32 [9216, 256], P('grp'), may hold values from 0.01 to 1
- gains: float32 [2, 1024], P(None, 'grp'), may hold values from 0.5 to 1.5
- gain_first: float32 [2, 1024], P(None, 'grp'), may hold values from -12 to 12
- gain_second: float32 [2, 1024], P(None, 'grp'), may hold values from 0.01 to 1
Outputs:
- new_weights: float32 [1024, 9216], P('grp')
- new_first: float32 [9216, 256], P('grp')
- new_second: float32 [9216, 256], P('grp')
- new_basis: float32 [1024, 256], P('grp')
- new_gains: float32 [2, 1024], P(None, 'grp')
- new_gain_first: float32 [2, 1024], P(None, 'grp')
- new_gain_second: float32 [2, 1024], P(None, 'grp')
All inputs are finite; a program needn't handle non-finite values.
Results may differ from a plain program's by a relative error of at most 0.0001.
Values sent between devices are 32-bit elements; how exact they have to be, the bound alone decides.
A program may use at most 64 MiB of HBM per device.

v0:
```python
import jax
import jax.numpy as jnp
from jax import lax
from jax.sharding import PartitionSpec as P

NS_STEPS = 3


beta_first = 0.9
beta_second = 0.999
learn_rate = 0.1
galore_scale = 0.25
adam_eps = 1e-08


def exact_dot(left, right):
    return jnp.dot(left, right, precision=lax.Precision.HIGHEST, preferred_element_type=jnp.float32)


def body(
    grad_parts,
    gain_grad_parts,
    weights,
    basis,
    moment_first,
    moment_second,
    gains,
    gain_first,
    gain_second,
):
    corr_first = 1.0 - beta_first**10
    corr_second = 1.0 - beta_second**10
    local_grad = grad_parts[0]
    local_gain = gain_grad_parts[0]
    source, gain_grad = lax.psum((local_grad, local_gain), "rep")
    col_block = lax.all_to_all(source, "grp", split_axis=1, concat_axis=0, tiled=True)
    full_basis = lax.all_gather(basis, "grp", axis=0, tiled=True)
    projected = exact_dot(col_block.T, full_basis)
    new_first = beta_first * moment_first + (1.0 - beta_first) * projected
    new_second = beta_second * moment_second + (1.0 - beta_second) * projected * projected
    direction = new_first / corr_first / (jnp.sqrt(new_second / corr_second) + adam_eps)
    subspace = lax.psum_scatter(
        exact_dot(col_block, projected), "grp", scatter_dimension=0, tiled=True
    )
    update_cols = exact_dot(full_basis, direction.T)
    update = lax.all_to_all(update_cols, "grp", split_axis=0, concat_axis=1, tiled=True)
    new_weights = weights - learn_rate * galore_scale * update
    gram = lax.psum(exact_dot(subspace.T, subspace), "grp")
    scale = jnp.sqrt(jnp.sqrt(jnp.sum(gram * gram) + 1e-06))
    iterate = subspace / scale
    current = lax.psum(exact_dot(iterate.T, iterate), "grp")
    for step in range(NS_STEPS):
        iterate = 1.5 * iterate - 0.5 * exact_dot(iterate, current)
        if step + 1 < NS_STEPS:
            current = lax.psum(exact_dot(iterate.T, iterate), "grp")
    new_gain_first = beta_first * gain_first + (1.0 - beta_first) * gain_grad
    new_gain_second = beta_second * gain_second + (1.0 - beta_second) * gain_grad * gain_grad
    new_gains = gains - learn_rate * (new_gain_first / corr_first) / (
        jnp.sqrt(new_gain_second / corr_second) + adam_eps
    )
    return (new_weights, new_first, new_second, iterate, new_gains, new_gain_first, new_gain_second)


def solution(mesh):
    in_specs = (
        P("rep", "grp", None),
        P("rep", None, "grp"),
        P("grp", None),
        P("grp", None),
        P("grp", None),
        P("grp", None),
        P(None, "grp"),
        P(None, "grp"),
        P(None, "grp"),
    )
    out_specs = (
        P("grp", None),
        P("grp", None),
        P("grp", None),
        P("grp", None),
        P(None, "grp"),
        P(None, "grp"),
        P(None, "grp"),
    )
    return jax.shard_map(body, mesh=mesh, in_specs=in_specs, out_specs=out_specs, check_vma=False)
```

profile of v0, /device:TPU:17, one launch (start us, length us, event | category | flops | bytes accessed | tf_op | source)
XLA Modules:
  0.0 693.5 jit_solution(16123633923945637209)
XLA Ops:
  8.0 0.0 all-reduce.6.cloned.1.call-start
  8.0 2.2 all_to_all.24
  10.2 2.3 copy.34
  12.5 0.0 all-reduce.6.cloned.1.call-update
  12.6 24.2 %all-reduce.6.cloned.1.call-done = f32[64,16,576]{2,0,1:T(8,128)} async-done(((f32[64,16,576]{2,0,1:T(8,128)}), f32[64,16,576]{2,0,1:T(8,128)}) %all-reduce.6.cloned.1.call-update) | async-done | bytes 2359312 | tf_op jit(solution)/shard_map/psum | solution.py:35
  36.8 6.4 all-to-all-start
  43.2 0.0 all-gather.2.cloned.1.call-start
  43.2 0.5 all-gather.2.cloned.1.call-update
  43.7 0.0 reduce-scatter.4.cloned.1.call-start
  43.8 79.3 %all-gather.2.cloned.1.call-done = f32[1024,256]{1,0:T(8,128)} async-done(((f32[64,256]{1,0:T(8,128)}), f32[1024,256]{1,0:T(8,128)}) %all-gather.2.cloned.1.call-update) | async-done | bytes 1048592 | tf_op jit(solution)/shard_map/all_gather | solution.py:37
  123.1 6.7 multiply_add_fusion
  129.8 5.5 convolution_bitcast_fusion.1
  135.3 2.6 copy.38
  137.9 0.0 reduce-scatter.4.cloned.1.call-update
  137.9 3.8 convolution_bitcast_fusion
  141.7 2.1 copy.35
  143.8 5.4 all-to-all-start.1
  149.2 0.0 copy-start.1
  149.2 0.0 copy-start.2
  149.2 0.0 copy-start.3
  149.2 0.0 all-reduce.8.cloned.1.call-start
  149.3 67.4 %reduce-scatter.4.cloned.1.call-done = f32[64,256]{1,0:T(8,128)} async-done(((f32[1024,256]{1,0:T(8,128)}), f32[64,256]{1,0:T(8,128)}) %reduce-scatter.4.cloned.1.call-update) | async-done | bytes 65552
  216.7 2.0 fusion.18
  218.8 0.0 all-reduce.8.cloned.1.call-update
  218.8 0.2 all-reduce.10.cloned.1.call-start
  219.0 121.5 %all-reduce.8.cloned.1.call-done = f32[256,256]{1,0:T(8,128)} async-done(((f32[256,256]{1,0:T(8,128)}), f32[256,256]{1,0:T(8,128)}) %all-reduce.8.cloned.1.call-update) | async-done | bytes 262160 | tf_op jit(solution)/shard_map/psum | solution.py:48
  340.5 1.6 multiply_reduce_fusion
  342.9 2.0 fusion.12
  344.9 0.0 all-reduce.10.cloned.1.call-update
  345.0 0.0 all-reduce.12.cloned.1.call-start
  345.0 107.5 %all-reduce.10.cloned.1.call-done = f32[256,256]{1,0:T(8,128)} async-done(((f32[256,256]{1,0:T(8,128)}), f32[256,256]{1,0:T(8,128)}) %all-reduce.10.cloned.1.call-update) | async-done | bytes 262160 | tf_op jit(solution)/shard_map/psum | solution.py:51
  452.5 1.2 fusion.2
  453.7 1.1 fusion.19
  454.8 0.0 all-reduce.12.cloned.1.call-update
  454.9 0.0 all-reduce.14.cloned.1.call-start
  454.9 109.6 %all-reduce.12.cloned.1.call-done = f32[256,256]{1,0:T(8,128)} async-done(((f32[256,256]{1,0:T(8,128)}), f32[256,256]{1,0:T(8,128)}) %all-reduce.12.cloned.1.call-update) | async-done | bytes 262160 | tf_op jit(solution)/shard_map/psum | solution.py:55
  564.5 1.2 fusion.1
  565.7 1.1 fusion.20
  566.8 0.0 all-reduce.14.cloned.1.call-update
  566.8 4.8 psum.47
  571.6 0.6 divide_subtract_fusion
  572.2 104.3 %all-reduce.14.cloned.1.call-done = f32[256,256]{1,0:T(8,128)} async-done(((f32[256,256]{1,0:T(8,128)}), f32[256,256]{1,0:T(8,128)}) %all-reduce.14.cloned.1.call-update) | async-done | bytes 262160 | tf_op jit(solution)/shard_map/psum | solution.py:55
  676.5 1.8 fusion
  678.3 0.0 all-to-all-done.1
  678.3 0.2 multiply_bitcast_fusion
  678.5 1.5 copy.36
  680.1 2.0 mul.101
  682.1 4.0 sub.15
  (8 shorter events, 0.0 us)
Async XLA Ops:
  8.0 28.8 %all-reduce.6.cloned.1.call-start = ((), (), s32[]{:S(2)}) async-start(), calls=%async_computation.3 | async-start | bytes 5242880 | tf_op jit(solution)/shard_map/psum | solution.py:35
  36.8 86.4 %all-to-all-start = ((f32[64,16,576]{2,0,1:T(8,128)}), f32[64,16,576]{2,0,1:T(8,128)S(1)}, u32[]{:S(2)}, u32[]{:S(2)}) async-start(f32[64,16,576]{2,0,1:T(8,128)} %all-reduce.6.cloned.1.call-done), calls=%async_computation | async-start | bytes 5242880 | tf_op jit(solution)/shard_map/all_to_all | solution.py:36
  43.2 80.0 %all-gather.2.cloned.1.call-start = ((), (), s32[]{:S(2)}) async-start(), calls=%async_computation.4 | async-start | bytes 1114112 | tf_op jit(solution)/shard_map/all_gather | solution.py:37
  43.7 173.0 %reduce-scatter.4.cloned.1.call-start = ((), (), s32[]{:S(2)}) async-start(), calls=%async_computation.9 | async-start | bytes 1114112
  129.8 8.1 %copy-start = (f32[576,256]{1,0:T(8,128)}, f32[576,256]{1,0:T(8,128)S(1)}, u32[]{:S(2)}) copy-start(f32[576,256]{1,0:T(8,128)S(1)} %get-tuple-element.31) | copy-start | bytes 1769476
  143.8 534.5 %all-to-all-start.1 = ((f32[16,64,576]{2,1,0:T(8,128)}), f32[16,64,576]{2,1,0:T(8,128)S(1)}, u32[]{:S(2)}, u32[]{:S(2)}) async-start(f32[16,64,576]{2,1,0:T(8,128)} %bitcast.30), calls=%async_computation.1 | async-start | bytes 5242880 | tf_op jit(solution)/shard_map/all_to_all | solution.py:46
  149.2 417.6 %copy-start.4 = (f32[1,2,64]{2,1,0:T(2,128)S(1)}, f32[1,2,64]{2,1,0:T(2,128)}, u32[]{:S(2)}) copy-start(f32[1,2,64]{2,1,0:T(2,128)} %param.10) | copy-start | bytes 1540
  149.2 422.4 %copy-start.1 = (f32[2,64]{1,0:T(2,128)S(1)}, f32[2,64]{1,0:T(2,128)}, u32[]{:S(2)}) copy-start(f32[2,64]{1,0:T(2,128)} %param.15) | copy-start | bytes 1540
  149.2 422.4 %copy-start.2 = (f32[2,64]{1,0:T(2,128)S(1)}, f32[2,64]{1,0:T(2,128)}, u32[]{:S(2)}) copy-start(f32[2,64]{1,0:T(2,128)} %param.16) | copy-start | bytes 1540
  149.2 422.4 %copy-start.3 = (f32[2,64]{1,0:T(2,128)S(1)}, f32[2,64]{1,0:T(2,128)}, u32[]{:S(2)}) copy-start(f32[2,64]{1,0:T(2,128)} %param.17) | copy-start | bytes 1540
  149.2 191.3 %all-reduce.8.cloned.1.call-start = ((), (), s32[]{:S(2)}) async-start(), calls=%async_computation.5 | async-start | bytes 524288 | tf_op jit(solution)/shard_map/psum | solution.py:48
  218.8 233.7 %all-reduce.10.cloned.1.call-start = ((), (), s32[]{:S(2)}) async-start(), calls=%async_computation.6 | async-start | bytes 524288 | tf_op jit(solution)/shard_map/psum | solution.py:51
  345.0 219.5 %all-reduce.12.cloned.1.call-start = ((), (), s32[]{:S(2)}) async-start(), calls=%async_computation.7 | async-start | bytes 524288 | tf_op jit(solution)/shard_map/psum | solution.py:55
  454.9 221.6 %all-reduce.14.cloned.1.call-start = ((), (), s32[]{:S(2)}) async-start(), calls=%async_computation.8 | async-start | bytes 524288 | tf_op jit(solution)/shard_map/psum | solution.py:55
Sparse Core Ops, SparseCore 0:
  12.7 24.0 all-reduce.5
Sparse Core Ops, SparseCore 1:
  46.4 76.7 all-gather.1
  138.0 78.7 reduce-scatter.3
  222.4 118.1 all-reduce.7
  346.3 106.1 all-reduce.9
  458.3 106.1 all-reduce.11
  570.3 106.1 all-reduce.13
where the time goes:
time: 699 us; the launch traced here: 694 us
  waiting for transfers between devices  614 us (88%)
  matrix products  26.5 us (4%)
  between operations  16.4 us (2%)
  local copies, waits for them, and re-layouts  12.7 us (2%)
  starting transfers between devices  12.3 us (2%)
    psum x3, waiting for transfers between devices, body(): current = lax.psum(exact_dot(iterate.T, iterate), 'grp')  321 us
    psum x1, waiting for transfers between devices, body(): gram = lax.psum(exact_dot(subspace.T, subspace), 'grp')  122 us
    all_gather x1, waiting for transfers between devices, body(): full_basis = lax.all_gather(basis, 'grp', axis=0, tiled=True)  79.3 us
    unnamed x8, waiting for transfers between devices  68 us
    dot_general x10, matrix products, exact_dot(): jnp.dot(left, right, precision=lax.Precision.HIGHEST, preferred_element_t...  26.5 us
    psum x1, waiting for transfers between devices, body(): source, gain_grad = lax.psum((local_grad, local_gain), 'rep')  24.2 us
  transfers between devices with their start and end apart: 9, of which 7 were waited for; matrix products, arithmetic and copies ran while one was open for 3% of the time, Pallas kernels for 0%

commit v1 on v0

--- a/solution.py
+++ b/solution.py
@@ -30,29 +30,61 @@
 ):
     corr_first = 1.0 - beta_first**10
     corr_second = 1.0 - beta_second**10
+    n = lax.axis_size("grp")
+    rep = lax.axis_index("rep")
+    swap = [(0, 1), (1, 0)]
     local_grad = grad_parts[0]
     local_gain = gain_grad_parts[0]
-    source, gain_grad = lax.psum((local_grad, local_gain), "rep")
+    rows, ncol = local_grad.shape
+    half = rows // 2
+    block = ncol // n
+    rank = basis.shape[1]
+
+    def own_half(x):
+        return lax.dynamic_slice_in_dim(x, rep * half, half, 0)
+
+    def other_half(x):
+        return lax.dynamic_slice_in_dim(x, (1 - rep) * half, half, 0)
+
+    def swapped(x):
+        return lax.ppermute(x, "rep", swap)
+
+    def joined(mine, other):
+        return jnp.where(rep == 0, jnp.concatenate([mine, other], 0), jnp.concatenate([other, mine], 0))
+
+    def exchange(x):
+        return lax.all_to_all(x, "grp", split_axis=0, concat_axis=0, tiled=True)
+
+    def gathered(x):
+        return exchange(jnp.tile(x, (n, 1)))
+
+    half_basis = gathered(own_half(basis))
+    source = own_half(local_grad) + swapped(other_half(local_grad))
+    gain_grad = local_gain + swapped(local_gain)
     col_block = lax.all_to_all(source, "grp", split_axis=1, concat_axis=0, tiled=True)
-    full_basis = lax.all_gather(basis, "grp", axis=0, tiled=True)
-    projected = exact_dot(col_block.T, full_basis)
+    partial = exact_dot(col_block.T, half_basis)
+    projected = partial + swapped(partial)
     new_first = beta_first * moment_first + (1.0 - beta_first) * projected
     new_second = beta_second * moment_second + (1.0 - beta_second) * projected * projected
     direction = new_first / corr_first / (jnp.sqrt(new_second / corr_second) + adam_eps)
-    subspace = lax.psum_scatter(
-        exact_dot(col_block, projected), "grp", scatter_dimension=0, tiled=True
-    )
-    update_cols = exact_dot(full_basis, direction.T)
+    terms = exchange(exact_dot(col_block, projected))
+    sub_half = jnp.sum(terms.reshape(n, half, rank), axis=0)
+    sub_all = gathered(sub_half)
+    gram_half = exact_dot(sub_all.T, sub_all)
+    gram = gram_half + swapped(gram_half)
+    subspace = joined(sub_half, swapped(sub_half))
+    update_cols = exact_dot(half_basis, direction.T)
     update = lax.all_to_all(update_cols, "grp", split_axis=0, concat_axis=1, tiled=True)
-    new_weights = weights - learn_rate * galore_scale * update
-    gram = lax.psum(exact_dot(subspace.T, subspace), "grp")
+    new_half = own_half(weights) - learn_rate * galore_scale * update
+    new_weights = joined(new_half, swapped(new_half))
     scale = jnp.sqrt(jnp.sqrt(jnp.sum(gram * gram) + 1e-06))
     iterate = subspace / scale
-    current = lax.psum(exact_dot(iterate.T, iterate), "grp")
+    current = gram / scale / scale
     for step in range(NS_STEPS):
         iterate = 1.5 * iterate - 0.5 * exact_dot(iterate, current)
         if step + 1 < NS_STEPS:
-            current = lax.psum(exact_dot(iterate.T, iterate), "grp")
+            side = 1.5 * current - 0.5 * exact_dot(current, current)
+            current = 1.5 * side - 0.5 * exact_dot(side, current)
     new_gain_first = beta_first * gain_first + (1.0 - beta_first) * gain_grad
     new_gain_second = beta_second * gain_second + (1.0 - beta_second) * gain_grad * gain_grad
     new_gains = gains - learn_rate * (new_gain_first / corr_first) / (

time: 699 us -> 150 us (0.21)
  waiting for transfers between devices: 614 us -> 44.7 us
  blocking collectives: 4.76 us -> 53.2 us
  matrix products: 26.5 us -> 11.5 us
  between operations: 16.4 us -> 1.58 us
  starting transfers between devices: 12.3 us -> 23.7 us
    psum x5 -> x0, waiting for transfers between devices: 467 us -> none  [the longest x3 321 us: body(): current = lax.psum(exact_dot(iterate.T, iterate), 'grp')]
    all_gather x1 -> x0, waiting for transfers between devices: 79.3 us -> none  [body(): full_basis = lax.all_gather(basis, 'grp', axis=0, tiled=True)]
    unnamed x8 -> x0, waiting for transfers between devices: 68 us -> none
    all_to_all x0 -> x2, blocking collectives: none -> 53.2 us  [the longest x1 35.1 us: body(): lax.all_to_all(source, 'grp', split_axis=1, concat_axis=0, tiled=True)]
    all_to_all x1, waiting for transfers between devices: 0.01 us -> 23.4 us  [body(): lax.all_to_all(update_cols, 'grp', split_axis=0, concat_axis=1, tiled=True)]
    all_to_all x1 -> x2, waiting for transfers between devices: 0.01 us -> 18.9 us  [exchange(): return lax.all_to_all(x, 'grp', split_axis=0, concat_axis=0, tiled=True)]
    dot_general x10 -> x11, matrix products: 26.5 us -> 11.5 us  [exact_dot(): jnp.dot(left, right, precision=lax.Precision.HIGHEST, preferred_element_t...]
  transfers between devices with their start and end apart: 9 -> 9, of which waited for: 7 -> 5; matrix products, arithmetic and copies ran while one was open for 3% -> 11% of each run, Pallas kernels for 0% -> 0%
where the time goes in v1:
time: 150 us; the launch traced here: 148 us
  blocking collectives  53.2 us (35%)
  waiting for transfers between devices  44.7 us (30%)
  starting transfers between devices  23.7 us (16%)
  matrix products  11.5 us (8%)
  other arithmetic  7.11 us (5%)
  local copies, waits for them, and re-layouts  6.02 us (4%)
  between operations  1.58 us (1%)
    all_to_all x1, blocking collectives, body(): lax.all_to_all(source, 'grp', split_axis=1, concat_axis=0, tiled=True)  35.1 us
    all_to_all x1, waiting for transfers between devices, body(): lax.all_to_all(update_cols, 'grp', split_axis=0, concat_axis=1, tiled=True)  23.4 us
    all_to_all x2, waiting for transfers between devices, exchange(): return lax.all_to_all(x, 'grp', split_axis=0, concat_axis=0, tiled=True)  18.9 us
    all_to_all x1, blocking collectives, exchange(): return lax.all_to_all(x, 'grp', split_axis=0, concat_axis=0, tiled=True)  18.1 us
    all_to_all x2, starting transfers between devices, exchange(): return lax.all_to_all(x, 'grp', split_axis=0, concat_axis=0, tiled=True)  11.7 us
    dot_general x11, matrix products, exact_dot(): jnp.dot(left, right, precision=lax.Precision.HIGHEST, preferred_element_t...  11.5 us
    ppermute x6, starting transfers between devices, swapped(): return lax.ppermute(x, 'rep', swap)  6.61 us
    all_to_all x1, starting transfers between devices, body(): lax.all_to_all(update_cols, 'grp', split_axis=0, concat_axis=1, tiled=True)  5.31 us
  transfers between devices with their start and end apart: 9, of which 5 were waited for; matrix products, arithmetic and copies ran while one was open for 11% of the time, Pallas kernels for 0%

profile of v1, /device:TPU:17, one launch (start us, length us, event | category | flops | bytes accessed | tf_op | source)
XLA Modules:
  0.0 147.8 jit_solution(4049808414563732338)
XLA Ops:
  0.6 0.0 copy-start
  0.7 1.4 dynamic-slice_bitcast_fusion
  2.0 0.7 collective-permute-start
  2.8 0.8 tile.4
  3.6 6.6 %all-to-all-start = ((f32[16,32,256]{2,1,0:T(8,128)}), f32[16,32,256]{2,1,0:T(8,128)S(1)}, u32[]{:S(2)}, u32[]{:S(2)}) async-start(f32[16,32,256]{2,1,0:T(8,128)} %tile.4), calls=%async_computation | async-start | bytes 1048576 | tf_op jit(solution)/shard_map/all_to_all | solution.py:56
  10.2 0.0 collective-permute-done
  10.2 1.4 bitcast_add_fusion
  11.6 0.4 all_to_all.33
  12.0 0.4 copy.16
  12.5 10.8 %all-to-all-done = f32[16,32,256]{2,1,0:T(8,128)S(1)} async-done(((f32[16,32,256]{2,1,0:T(8,128)}), f32[16,32,256]{2,1,0:T(8,128)S(1)}, u32[]{:S(2)}, u32[]{:S(2)}) %all-to-all-start) | async-done | bytes 524320 | tf_op jit(solution)/shard_map/all_to_all | solution.py:56
  23.3 35.1 %all_to_all.44 = f32[32,16,576]{2,0,1:T(8,128)S(1)} all-to-all(f32[32,16,576]{2,0,1:T(8,128)S(1)} %copy.16), channel_id=1, replica_groups=mesh['rep'=2,'grp'=16] {'grp'}, dimensions={1} | all-to-all | bytes 2359296 | tf_op jit(solution)/shard_map/all_to_all | solution.py:64
  58.4 2.2 %fusion.4 = f32[576,256]{1,0:T(8,128)S(1)} fusion(f32[16,32,256]{2,1,0:T(8,128)S(1)} %all-to-all-done, f32[32,16,576]{2,0,1:T(8,128)S(1)} %all_to_all.44), kind=kOutput, calls=%fused_computation.6 | convolution fusion | flops 905969664 | bytes 2293760 | tf_op jit(solution)/shard_map/dot_general | solution.py:17
  60.6 1.4 collective-permute-start.1
  62.0 1.6 %collective-permute-done.1 = f32[576,256]{1,0:T(8,128)S(1)} collective-permute-done((f32[576,256]{1,0:T(8,128)S(1)}, f32[576,256]{1,0:T(8,128)S(1)}, u32[]{:S(2)}, u32[]{:S(2)}) %collective-permute-start.1) | collective-permute-done | bytes 589856 | tf_op jit(solution)/shard_map/ppermute | solution.py:50
  63.6 1.4 fusion
  65.0 18.1 %all_to_all.45 = f32[16,32,256]{2,1,0:T(8,128)S(1)} all-to-all(f32[16,32,256]{2,1,0:T(8,128)S(1)} %fusion), channel_id=1, replica_groups=mesh['rep'=2,'grp'=16] {'grp'}, dimensions={0} | all-to-all | bytes 1048576 | tf_op jit(solution)/shard_map/all_to_all | solution.py:56
  83.2 0.8 tile.5
  84.1 5.2 %all-to-all-start.4 = ((f32[16,32,256]{2,1,0:T(8,128)}), f32[16,32,256]{2,1,0:T(8,128)}, u32[]{:S(2)}, u32[]{:S(2)}) async-start(f32[16,32,256]{2,1,0:T(8,128)} %tile.5), calls=%async_computation.4 | async-start | bytes 1048576 | tf_op jit(solution)/shard_map/all_to_all | solution.py:56
  89.3 0.0 copy-start.4
  89.3 1.3 multiply_add_fusion
  90.6 0.0 copy-start.2
  90.6 0.0 copy-start.1
  90.6 0.8 copy-done.2
  91.4 2.7 %fusion.13 = f32[16,32,576]{2,1,0:T(8,128)} fusion(f32[16,32,256]{2,1,0:T(8,128)S(1)} %copy-done.4, f32[576,256]{1,0:T(8,128)S(1)} %get-tuple-element.13, f32[576,256]{1,0:T(8,128)S(1)} %get-tuple-element.12), kind=kOutput, calls=%fused_computation.25 | convolution fusion | flops 906559488 | bytes 2883584 | tf_op jit(solution)/shard_map/dot_general | solution.py:17
  94.2 0.0 copy-start.9
  94.2 8.0 %all-to-all-done.4 = f32[16,32,256]{2,1,0:T(8,128)} async-done(((f32[16,32,256]{2,1,0:T(8,128)}), f32[16,32,256]{2,1,0:T(8,128)}, u32[]{:S(2)}, u32[]{:S(2)}) %all-to-all-start.4) | async-done | bytes 524320 | tf_op jit(solution)/shard_map/all_to_all | solution.py:56
  102.2 5.3 %all-to-all-start.2 = ((f32[16,32,576]{2,1,0:T(8,128)}), f32[16,32,576]{2,1,0:T(8,128)S(1)}, u32[]{:S(2)}, u32[]{:S(2)}) async-start(f32[16,32,576]{2,1,0:T(8,128)} %fusion.13), calls=%async_computation.2 | async-start | bytes 2621440 | tf_op jit(solution)/shard_map/all_to_all | solution.py:77
  107.5 2.2 %collective-permute-start.5 = (f32[2,64]{1,0:T(2,128)S(1)}, f32[2,64]{1,0:T(2,128)S(1)}, u32[]{:S(2)}, u32[]{:S(2)}) collective-permute-start(f32[2,64]{1,0:T(2,128)S(1)} %bitcast.39), channel_id=1, source_target_pairs={{0,16},{16,0},{1,17},{17,1},{2,18},{18,2},{3,19},{19,3},{4,20},{20... | collective-permute-start | bytes 1544 | tf_op jit(solution)/shard_map/ppermute | solution.py:50
  109.7 0.8 collective-permute-done.5
  110.5 0.6 divide_subtract_fusion
  111.1 0.3 collective-permute-start.3
  111.5 2.2 %convolution_bitcast_fusion = f32[256,256]{1,0:T(8,128)S(1)} fusion(f32[16,32,256]{2,1,0:T(8,128)} %all-to-all-done.4), kind=kOutput, calls=%fused_computation.16 | convolution fusion | flops 402653184 | bytes 786432 | tf_op jit(solution)/shard_map/dot_general | solution.py:17
  113.7 0.2 collective-permute-start.4
  113.9 23.4 %all-to-all-done.2 = f32[16,32,576]{2,1,0:T(8,128)S(1)} async-done(((f32[16,32,576]{2,1,0:T(8,128)}), f32[16,32,576]{2,1,0:T(8,128)S(1)}, u32[]{:S(2)}, u32[]{:S(2)}) %all-to-all-start.2) | async-done | bytes 1179680 | tf_op jit(solution)/shard_map/all_to_all | solution.py:77
  137.3 0.1 multiply_bitcast_fusion
  137.4 0.8 copy.17
  138.2 0.5 mul.135
  138.7 1.4 dynamic-slice_subtract_fusion
  140.1 1.7 %collective-permute-start.2 = (f32[32,9216]{1,0:T(8,128)S(1)}, f32[32,9216]{1,0:T(8,128)S(1)}, u32[]{:S(2)}, u32[]{:S(2)}) collective-permute-start(f32[32,9216]{1,0:T(8,128)S(1)} %dynamic-slice_subtract_fusion), channel_id=1, source_target_pairs={{0,16},{16,0},{1,17},{17,1},{2,18},{18,2},{3,19},{19,3},{4,20},{20... | collective-permute-start | bytes 3538952 | tf_op jit(solution)/shard_map/ppermute | solution.py:50
  141.8 0.7 multiply_reduce_fusion
  143.2 0.4 convolution_multiply_fusion.3
  143.6 0.4 multiply_subtract_fusion
  144.0 0.3 convolution_multiply_fusion.6
  144.3 0.3 fusion.10
  144.6 0.4 fusion.8
  145.0 0.4 fusion.7
  145.3 0.9 fusion.9
  146.2 1.6 %maximum_select_fusion = f32[64,9216]{1,0:T(8,128)} fusion(f32[32,9216]{1,0:T(8,128)S(1)} %collective-permute-done.2, f32[32,9216]{1,0:T(8,128)S(1)} %dynamic-slice_subtract_fusion, pred[]{:T(512)S(6)} %eq.4), kind=kLoop, calls=%fused_computation | loop fusion | flops 1769472 | bytes 4718593 | tf_op jit(solution)/shard_map/jit(_where)/select_n | solution.py:53
  (19 shorter events, 0.1 us)
Async XLA Ops:
  0.6 2.2 %copy-start = (f32[64,256]{1,0:T(8,128)S(1)}, f32[64,256]{1,0:T(8,128)}, u32[]{:S(2)}) copy-start(f32[64,256]{1,0:T(8,128)} %param.12) | copy-start | bytes 196612
  2.0 8.2 %collective-permute-start = (f32[32,9216]{1,0:T(8,128)S(1)}, f32[32,9216]{1,0:T(8,128)S(1)}, u32[]{:S(2)}, u32[]{:S(2)}) collective-permute-start(f32[32,9216]{1,0:T(8,128)S(1)} %dynamic-slice_bitcast_fusion), channel_id=1, source_target_pairs={{0,16},{16,0},{1,17},{17,1},{2,18},{18,2},{3,19},{19,3},{4,20},{20... | collective-permute-start | bytes 3538952 | tf_op jit(solution)/shard_map/ppermute | solution.py:50
  3.6 19.7 %all-to-all-start = ((f32[16,32,256]{2,1,0:T(8,128)}), f32[16,32,256]{2,1,0:T(8,128)S(1)}, u32[]{:S(2)}, u32[]{:S(2)}) async-start(f32[16,32,256]{2,1,0:T(8,128)} %tile.4), calls=%async_computation | async-start | bytes 1048576 | tf_op jit(solution)/shard_map/all_to_all | solution.py:56
  23.3 35.1 %copy-start.3 = (f32[16,32,256]{2,1,0:T(8,128)}, f32[16,32,256]{2,1,0:T(8,128)S(1)}, u32[]{:S(2)}) copy-start(f32[16,32,256]{2,1,0:T(8,128)S(1)} %all-to-all-done) | copy-start | bytes 1572868
  60.6 3.0 %collective-permute-start.1 = (f32[576,256]{1,0:T(8,128)S(1)}, f32[576,256]{1,0:T(8,128)S(1)}, u32[]{:S(2)}, u32[]{:S(2)}) collective-permute-start(f32[576,256]{1,0:T(8,128)S(1)} %fusion.4), channel_id=1, source_target_pairs={{0,16},{16,0},{1,17},{17,1},{2,18},{18,2},{3,19},{19,3},{4,20},{20... | collective-permute-start | bytes 1769480 | tf_op jit(solution)/shard_map/ppermute | solution.py:50
  83.2 6.1 %copy-start.5 = (f32[576,256]{1,0:T(8,128)S(1)}, f32[576,256]{1,0:T(8,128)}, u32[]{:S(2)}) copy-start(f32[576,256]{1,0:T(8,128)} %param.13) | copy-start | bytes 1769476
  84.1 18.1 %all-to-all-start.4 = ((f32[16,32,256]{2,1,0:T(8,128)}), f32[16,32,256]{2,1,0:T(8,128)}, u32[]{:S(2)}, u32[]{:S(2)}) async-start(f32[16,32,256]{2,1,0:T(8,128)} %tile.5), calls=%async_computation.4 | async-start | bytes 1048576 | tf_op jit(solution)/shard_map/all_to_all | solution.py:56
  89.3 2.2 %copy-start.4 = (f32[16,32,256]{2,1,0:T(8,128)S(1)}, f32[16,32,256]{2,1,0:T(8,128)}, u32[]{:S(2)}) copy-start(f32[16,32,256]{2,1,0:T(8,128)} %copy-done.3) | copy-start | bytes 1572868
  90.6 0.8 copy-start.2
  90.6 3.6 %copy-start.1 = (f32[576,256]{1,0:T(8,128)}, f32[576,256]{1,0:T(8,128)S(1)}, u32[]{:S(2)}) copy-start(f32[576,256]{1,0:T(8,128)S(1)} %get-tuple-element.12) | copy-start | bytes 1769476
  94.1 13.4 %copy-start.7 = (f32[1,2,64]{2,1,0:T(2,128)S(1)}, f32[1,2,64]{2,1,0:T(2,128)}, u32[]{:S(2)}) copy-start(f32[1,2,64]{2,1,0:T(2,128)} %param.10) | copy-start | bytes 1540
  94.2 16.4 %copy-start.6 = (f32[2,64]{1,0:T(2,128)S(1)}, f32[2,64]{1,0:T(2,128)}, u32[]{:S(2)}) copy-start(f32[2,64]{1,0:T(2,128)} %param.15) | copy-start | bytes 1540
  94.2 16.4 %copy-start.8 = (f32[2,64]{1,0:T(2,128)S(1)}, f32[2,64]{1,0:T(2,128)}, u32[]{:S(2)}) copy-start(f32[2,64]{1,0:T(2,128)} %param.16) | copy-start | bytes 1540
  94.2 16.4 %copy-start.9 = (f32[2,64]{1,0:T(2,128)S(1)}, f32[2,64]{1,0:T(2,128)}, u32[]{:S(2)}) copy-start(f32[2,64]{1,0:T(2,128)} %param.17) | copy-start | bytes 1540
  102.2 35.1 %all-to-all-start.2 = ((f32[16,32,576]{2,1,0:T(8,128)}), f32[16,32,576]{2,1,0:T(8,128)S(1)}, u32[]{:S(2)}, u32[]{:S(2)}) async-start(f32[16,32,576]{2,1,0:T(8,128)} %fusion.13), calls=%async_computation.2 | async-start | bytes 2621440 | tf_op jit(solution)/shard_map/all_to_all | solution.py:77
  107.5 3.0 %collective-permute-start.5 = (f32[2,64]{1,0:T(2,128)S(1)}, f32[2,64]{1,0:T(2,128)S(1)}, u32[]{:S(2)}, u32[]{:S(2)}) collective-permute-start(f32[2,64]{1,0:T(2,128)S(1)} %bitcast.39), channel_id=1, source_target_pairs={{0,16},{16,0},{1,17},{17,1},{2,18},{18,2},{3,19},{19,3},{4,20},{20... | collective-permute-start | bytes 1544 | tf_op jit(solution)/shard_map/ppermute | solution.py:50
  111.1 32.9 %collective-permute-start.3 = (f32[32,256]{1,0:T(8,128)S(1)}, f32[32,256]{1,0:T(8,128)S(1)}, u32[]{:S(2)}, u32[]{:S(2)}) collective-permute-start(f32[32,256]{1,0:T(8,128)S(1)} %reduce_sum.18), channel_id=1, source_target_pairs={{0,16},{16,0},{1,17},{17,1},{2,18},{18,2},{3,19},{19,3},{4,20},{20... | collective-permute-start | bytes 98312 | tf_op jit(solution)/shard_map/ppermute | solution.py:50
  113.7 28.1 %collective-permute-start.4 = (f32[256,256]{1,0:T(8,128)S(1)}, f32[256,256]{1,0:T(8,128)S(1)}, u32[]{:S(2)}, u32[]{:S(2)}) collective-permute-start(f32[256,256]{1,0:T(8,128)S(1)} %convolution_bitcast_fusion), channel_id=1, source_target_pairs={{0,16},{16,0},{1,17},{17,1},{2,18},{18,2},{3,19},{19,3},{4,20},{20... | collective-permute-start | bytes 786440 | tf_op jit(solution)/shard_map/ppermute | solution.py:50
  140.1 6.2 %collective-permute-start.2 = (f32[32,9216]{1,0:T(8,128)S(1)}, f32[32,9216]{1,0:T(8,128)S(1)}, u32[]{:S(2)}, u32[]{:S(2)}) collective-permute-start(f32[32,9216]{1,0:T(8,128)S(1)} %dynamic-slice_subtract_fusion), channel_id=1, source_target_pairs={{0,16},{16,0},{1,17},{17,1},{2,18},{18,2},{3,19},{19,3},{4,20},{20... | collective-permute-start | bytes 3538952 | tf_op jit(solution)/shard_map/ppermute | solution.py:50

commit v2 on v1

--- a/solution.py
+++ b/solution.py
@@ -1,6 +1,8 @@
 import jax
 import jax.numpy as jnp
 from jax import lax
+from jax.experimental import pallas as pl
+from jax.experimental.pallas import tpu as pltpu
 from jax.sharding import PartitionSpec as P
 
 NS_STEPS = 3
@@ -15,6 +17,139 @@
 
 def exact_dot(left, right):
     return jnp.dot(left, right, precision=lax.Precision.HIGHEST, preferred_element_type=jnp.float32)
+
+
+def far_first(n):
+    return sorted(range(1, n), key=lambda k: abs(k - n // 2))
+
+
+def peer_copy(src, dst, send_sem, recv_sem, where):
+    return pltpu.make_async_remote_copy(
+        src_ref=src,
+        dst_ref=dst,
+        send_sem=send_sem,
+        recv_sem=recv_sem,
+        device_id=where,
+        device_id_type=pl.DeviceIdType.MESH,
+    )
+
+
+def greet(others):
+    barrier = pltpu.get_barrier_semaphore()
+    for other in others:
+        pl.semaphore_signal(barrier, inc=1, device_id=other, device_id_type=pl.DeviceIdType.MESH)
+    pl.semaphore_wait(barrier, len(others))
+
+
+def scatter_grad(n, grad, basis, cols, full, swap, parts, swap_sems, basis_send, basis_recv, col_send, col_recv):
+    me, rep = lax.axis_index("grp"), lax.axis_index("rep")
+    half = swap.shape[0]
+    block = cols.shape[2]
+    offsets = far_first(n)
+    peers = {k: {"grp": lax.rem(me + k, n)} for k in offsets}
+    greet([{"rep": 1 - rep}] + [peers[k] for k in offsets])
+    own = pl.ds(pl.multiple_of(rep * half, half), half)
+    other = pl.ds(pl.multiple_of((1 - rep) * half, half), half)
+    trade = peer_copy(grad.at[other], swap, swap_sems.at[0], swap_sems.at[1], {"rep": 1 - rep})
+    trade.start()
+    copies = []
+    for k in offsets:
+        copies.append(peer_copy(basis.at[own], full.at[me], basis_send.at[k], basis_recv.at[k], peers[k]))
+        copies[-1].start()
+    full[pl.ds(me, 1)] = basis[own][None]
+    trade.wait()
+    for j in range(n):
+        parts[j] = grad[own, j * block : (j + 1) * block] + swap[:, j * block : (j + 1) * block]
+    cols[pl.ds(me, 1)] = parts[pl.ds(me, 1)]
+    for k in offsets:
+        target = peers[k]["grp"]
+        copies.append(peer_copy(parts.at[target], cols.at[me], col_send.at[k], col_recv.at[k], peers[k]))
+        copies[-1].start()
+    for copy in copies:
+        copy.wait()
+
+
+def reduce_and_return(n, terms, moved, rows, update, arrived, term_send, term_recv, row_send, row_recv, up_send, up_recv):
+    me = lax.axis_index("grp")
+    offsets = far_first(n)
+    peers = {k: {"grp": lax.rem(me + k, n)} for k in offsets}
+    greet([peers[k] for k in offsets])
+
+    def send_update(some):
+        for k in some:
+            copy = peer_copy(moved.at[peers[k]["grp"]], update.at[me], up_send.at[k], up_recv.at[k], peers[k])
+            copy.start()
+            late.append(copy)
+
+    late, early = [], []
+    for k in offsets:
+        copy = peer_copy(terms.at[peers[k]["grp"]], arrived.at[me], term_send.at[k], term_recv.at[k], peers[k])
+        copy.start()
+        early.append(copy)
+    first = n // 4
+    send_update(offsets[:first])
+    arrived[pl.ds(me, 1)] = terms[pl.ds(me, 1)]
+    update[pl.ds(me, 1)] = moved[pl.ds(me, 1)]
+    for copy in early:
+        copy.wait()
+    total = arrived[0]
+    for j in range(1, n):
+        total = total + arrived[j]
+    rows[pl.ds(me, 1)] = total[None]
+    send_update(offsets[first : first + 2])
+    for k in offsets:
+        copy = peer_copy(rows.at[me], rows.at[me], row_send.at[k], row_recv.at[k], peers[k])
+        copy.start()
+        late.append(copy)
+    send_update(offsets[first + 2 :])
+    for copy in late:
+        copy.wait()
+
+
+def in_vmem(count):
+    return [pl.BlockSpec(memory_space=pltpu.VMEM)] * count
+
+
+def call_scatter(n, grad, basis):
+    rows, ncol = grad.shape
+    half, block, rank = rows // 2, ncol // n, basis.shape[1]
+    sems = pltpu.SemaphoreType.DMA((n,))
+    return pl.pallas_call(
+        lambda *refs: scatter_grad(n, *refs),
+        out_shape=(
+            jax.ShapeDtypeStruct((n, half, block), jnp.float32),
+            jax.ShapeDtypeStruct((n, half, rank), jnp.float32),
+        ),
+        in_specs=in_vmem(2),
+        out_specs=tuple(in_vmem(2)),
+        scratch_shapes=[
+            pltpu.VMEM((half, ncol), jnp.float32),
+            pltpu.VMEM((n, half, block), jnp.float32),
+            pltpu.SemaphoreType.DMA((2,)),
+            sems,
+            sems,
+            sems,
+            sems,
+        ],
+        compiler_params=pltpu.CompilerParams(collective_id=0, has_side_effects=True),
+        name="scatter_grad",
+    )(grad, basis)
+
+
+def call_return(n, terms, moved):
+    sems = pltpu.SemaphoreType.DMA((n,))
+    return pl.pallas_call(
+        lambda *refs: reduce_and_return(n, *refs),
+        out_shape=(
+            jax.ShapeDtypeStruct(terms.shape, jnp.float32),
+            jax.ShapeDtypeStruct(moved.shape, jnp.float32),
+        ),
+        in_specs=in_vmem(2),
+        out_specs=tuple(in_vmem(2)),
+        scratch_shapes=[pltpu.VMEM(terms.shape, jnp.float32)] + [sems] * 6,
+        compiler_params=pltpu.CompilerParams(collective_id=1, has_side_effects=True),
+        name="reduce_and_return",
+    )(terms, moved)
 
 
 def body(
@@ -43,38 +178,30 @@
     def own_half(x):
         return lax.dynamic_slice_in_dim(x, rep * half, half, 0)
 
-    def other_half(x):
-        return lax.dynamic_slice_in_dim(x, (1 - rep) * half, half, 0)
-
     def swapped(x):
         return lax.ppermute(x, "rep", swap)
 
     def joined(mine, other):
         return jnp.where(rep == 0, jnp.concatenate([mine, other], 0), jnp.concatenate([other, mine], 0))
 
-    def exchange(x):
-        return lax.all_to_all(x, "grp", split_axis=0, concat_axis=0, tiled=True)
-
-    def gathered(x):
-        return exchange(jnp.tile(x, (n, 1)))
-
-    half_basis = gathered(own_half(basis))
-    source = own_half(local_grad) + swapped(other_half(local_grad))
     gain_grad = local_gain + swapped(local_gain)
-    col_block = lax.all_to_all(source, "grp", split_axis=1, concat_axis=0, tiled=True)
+    col_block, half_basis = call_scatter(n, local_grad, basis)
+    col_block = col_block.reshape(n * half, block)
+    half_basis = half_basis.reshape(n * half, rank)
     partial = exact_dot(col_block.T, half_basis)
     projected = partial + swapped(partial)
     new_first = beta_first * moment_first + (1.0 - beta_first) * projected
     new_second = beta_second * moment_second + (1.0 - beta_second) * projected * projected
     direction = new_first / corr_first / (jnp.sqrt(new_second / corr_second) + adam_eps)
-    terms = exchange(exact_dot(col_block, projected))
-    sub_half = jnp.sum(terms.reshape(n, half, rank), axis=0)
-    sub_all = gathered(sub_half)
+    terms = exact_dot(col_block, projected).reshape(n, half, rank)
+    update_cols = exact_dot(half_basis, direction.T).reshape(n, half, block)
+    sub_all, update = call_return(n, terms, update_cols)
+    sub_half = lax.dynamic_index_in_dim(sub_all, lax.axis_index("grp"), 0, keepdims=False)
+    sub_all = sub_all.reshape(n * half, rank)
+    update = jnp.swapaxes(update, 0, 1).reshape(half, ncol)
     gram_half = exact_dot(sub_all.T, sub_all)
     gram = gram_half + swapped(gram_half)
     subspace = joined(sub_half, swapped(sub_half))
-    update_cols = exact_dot(half_basis, direction.T)
-    update = lax.all_to_all(update_cols, "grp", split_axis=0, concat_axis=1, tiled=True)
     new_half = own_half(weights) - learn_rate * galore_scale * update
     new_weights = joined(new_half, swapped(new_half))
     scale = jnp.sqrt(jnp.sqrt(jnp.sum(gram * gram) + 1e-06))

time: 150 us -> 136 us (0.907)
  Pallas kernels: 0 us -> 106 us
  blocking collectives: 53.2 us -> 0 us
  waiting for transfers between devices: 44.7 us -> 1.55 us
  starting transfers between devices: 23.7 us -> 4.49 us
  local copies, waits for them, and re-layouts: 6.02 us -> 2.85 us
  other arithmetic: 7.11 us -> 4.56 us
  matrix products: 11.5 us -> 13.9 us
    pallas_call x0 -> x2, Pallas kernels: none -> 106 us  [the longest x1 58.2 us: call_return(): pl.pallas_call(lambda *refs: reduce_and_return(n, *refs), out_shape=(jax....]
    all_to_all x2 -> x0, blocking collectives: 53.2 us -> none  [the longest x1 35.1 us: body(): lax.all_to_all(source, 'grp', split_axis=1, concat_axis=0, tiled=True)]
    all_to_all x3 -> x0, waiting for transfers between devices: 42.2 us -> none  [the longest x1 23.4 us: body(): lax.all_to_all(update_cols, 'grp', split_axis=0, concat_axis=1, tiled=True)]
    all_to_all x3 -> x0, starting transfers between devices: 17.1 us -> none  [the longest x2 11.7 us: exchange(): return lax.all_to_all(x, 'grp', split_axis=0, concat_axis=0, tiled=True)]
    dot_general x11, matrix products: 11.5 us -> 13.9 us  [exact_dot(): jnp.dot(left, right, precision=lax.Precision.HIGHEST, preferred_element_t...]
    ppermute x6 -> x5, starting transfers between devices: 6.61 us -> 4.49 us  [swapped(): return lax.ppermute(x, 'rep', swap)]
    another operation x2 -> x0, local copies, waits for them, and re-layouts: 1.7 us -> none  [gathered(): return exchange(jnp.tile(x, (n, 1)))]
  transfers between devices with their start and end apart: 9 -> 5, of which waited for: 5 -> 1; matrix products, arithmetic and copies ran while one was open for 11% -> 6% of each run, Pallas kernels for 0% -> 0%
where the time goes in v2:
time: 136 us; the launch traced here: 135 us
  Pallas kernels  106 us (78%)
  matrix products  13.9 us (10%)
  other arithmetic  4.56 us (3%)
  starting transfers between devices  4.49 us (3%)
  local copies, waits for them, and re-layouts  2.85 us (2%)
  between operations  1.58 us (1%)
  waiting for transfers between devices  1.55 us (1%)
    pallas_call x1, Pallas kernels, call_return(): pl.pallas_call(lambda *refs: reduce_and_return(n, *refs), out_shape=(jax....  58.2 us
    pallas_call x1, Pallas kernels, call_scatter(): pl.pallas_call(lambda *refs: scatter_grad(n, *refs), out_shape=(jax.Shape...  47.6 us
    dot_general x11, matrix products, exact_dot(): jnp.dot(left, right, precision=lax.Precision.HIGHEST, preferred_element_t...  13.9 us
    ppermute x5, starting transfers between devices, swapped(): return lax.ppermute(x, 'rep', swap)  4.49 us
  transfers between devices with their start and end apart: 5, of which 1 were waited for; matrix products, arithmetic and copies ran while one was open for 6% of the time, Pallas kernels for 0%

profile of v2, /device:TPU:17, one launch (start us, length us, event | category | flops | bytes accessed | tf_op | source)
XLA Modules:
  0.0 134.8 jit_solution(13641275881932362349)
XLA Ops:
  0.6 47.6 %scatter_grad.1 = (f32[16,32,576]{2,1,0:T(8,128)}, f32[16,32,256]{2,1,0:T(8,128)}) custom-call(f32[64,9216]{1,0:T(8,128)} %bitcast.33, f32[64,256]{1,0:T(8,128)} %refs_1_.1), custom_call_target="tpu_custom_call" | custom-call | tf_op jit(solution)/shard_map/scatter_grad/pallas_call | solution.py:117
  48.2 0.0 copy-start.8
  48.2 0.0 copy-start.7
  48.2 0.0 copy-start.9
  48.3 0.0 copy-start.10
  48.3 0.0 copy-start.4
  48.3 0.0 copy-start.5
  48.3 3.7 %convolution_bitcast_fusion = f32[576,256]{1,0:T(8,128)S(1)} fusion(f32[16,32,576]{2,1,0:T(8,128)} %get-tuple-element.11, f32[16,32,256]{2,1,0:T(8,128)} %get-tuple-element.12), kind=kOutput, calls=%fused_computation.2 | convolution fusion | flops 905969664 | bytes 2293760 | tf_op jit(solution)/shard_map/dot_general | solution.py:19
  52.0 2.2 %collective-permute-start = (f32[576,256]{1,0:T(8,128)S(1)}, f32[576,256]{1,0:T(8,128)S(1)}, u32[]{:S(2)}, u32[]{:S(2)}) collective-permute-start(f32[576,256]{1,0:T(8,128)S(1)} %convolution_bitcast_fusion), channel_id=1, source_target_pairs={{0,16},{16,0},{1,17},{17,1},{2,18},{18,2},{3,19},{19,3},{4,20},{20... | collective-permute-start | bytes 1769480 | tf_op jit(solution)/shard_map/ppermute | solution.py:182
  54.3 0.0 copy-done.8
  54.3 0.1 collective-permute-start.4
  54.4 1.5 %collective-permute-done.4 = f32[2,64]{1,0:T(2,128)S(1)} collective-permute-done((f32[2,64]{1,0:T(2,128)S(1)}, f32[2,64]{1,0:T(2,128)S(1)}, u32[]{:S(2)}, u32[]{:S(2)}) %collective-permute-start.4) | collective-permute-done | bytes 544 | tf_op jit(solution)/shard_map/ppermute | solution.py:182
  55.9 0.0 copy-done.7
  55.9 0.0 copy-done.9
  55.9 0.0 copy-done.10
  55.9 0.6 divide_subtract_fusion
  56.5 0.0 collective-permute-done
  56.5 0.0 copy-done.4
  56.5 0.0 copy-done.5
  56.5 0.2 multiply_add_fusion
  56.7 0.0 copy-start
  56.7 0.0 copy-start.1
  56.7 0.8 copy-done.6
  57.5 2.7 %fusion.5.refs_1_ = f32[16,32,576]{2,1,0:T(8,128)} fusion(f32[16,32,256]{2,1,0:T(8,128)S(1)} %copy-done.6, f32[576,256]{1,0:T(8,128)S(1)} %get-tuple-element.21, f32[576,256]{1,0:T(8,128)S(1)} %get-tuple-element.20), kind=kOutput, calls=%fused_computation.18 | convolution fusion | flops 906559488 | bytes 2883584 | tf_op jit(solution)/shard_map/dot_general | solution.py:19
  60.3 0.0 copy-done.1
  60.3 2.2 %fusion.7.refs_0_ = f32[16,32,256]{2,1,0:T(8,128)} fusion(f32[16,32,576]{2,1,0:T(8,128)S(1)} %copy-done.2, f32[576,256]{1,0:T(8,128)S(1)} %convolution_bitcast_fusion, f32[576,256]{1,0:T(8,128)S(1)} %collective-permute-done), kind=kOutput, calls=%fused_computation.20 | convolution fusion | flops 906117120 | bytes 2883584 | tf_op jit(solution)/shard_map/dot_general | solution.py:19
  62.5 58.2 %reduce_and_return.1 = (f32[16,32,256]{2,1,0:T(8,128)}, f32[16,32,576]{2,1,0:T(8,128)}) custom-call(f32[16,32,256]{2,1,0:T(8,128)} %fusion.7.refs_0_, f32[16,32,576]{2,1,0:T(8,128)} %fusion.5.refs_1_), custom_call_target="tpu_custom_call" | custom-call | tf_op jit(solution)/shard_map/reduce_and_return/pallas_call | solution.py:141
  120.7 2.3 %convolution_bitcast_fusion.1 = f32[256,256]{1,0:T(8,128)S(1)} fusion(f32[16,32,256]{2,1,0:T(8,128)} %get-tuple-element.14), kind=kOutput, calls=%fused_computation.10 | convolution fusion | flops 402653184 | bytes 786432 | tf_op jit(solution)/shard_map/dot_general | solution.py:19
  123.1 1.6 %collective-permute-start.3 = (f32[256,256]{1,0:T(8,128)S(1)}, f32[256,256]{1,0:T(8,128)S(1)}, u32[]{:S(2)}, u32[]{:S(2)}) collective-permute-start(f32[256,256]{1,0:T(8,128)S(1)} %convolution_bitcast_fusion.1), channel_id=1, source_target_pairs={{0,16},{16,0},{1,17},{17,1},{2,18},{18,2},{3,19},{19,3},{4,20},{20... | collective-permute-start | bytes 786440 | tf_op jit(solution)/shard_map/ppermute | solution.py:182
  124.7 0.8 dynamic-slice_bitcast_fusion
  125.4 0.0 collective-permute-start.2
  125.4 0.1 multiply_bitcast_fusion
  125.6 0.8 copy.16
  126.3 0.5 mul.129
  126.8 1.4 %dynamic-slice_subtract_fusion = f32[32,9216]{1,0:T(8,128)S(1)} fusion(f32[32,9216]{1,0:T(8,128)S(1)} %mul.129, f32[64,9216]{1,0:T(8,128)} %param.11, s32[]{:T(128)S(6)} %select_n.24), kind=kLoop, calls=%fused_computation.3 | loop fusion | flops 294912 | bytes 3538948 | tf_op jit(solution)/shard_map/sub | solution.py:205
  128.2 0.6 collective-permute-start.1
  128.8 0.0 collective-permute-done.3
  128.8 0.7 multiply_reduce_fusion
  130.2 0.4 convolution_multiply_fusion.3
  130.6 0.4 multiply_subtract_fusion
  131.0 0.0 collective-permute-done.2
  131.0 0.3 convolution_multiply_fusion.6
  131.3 0.3 fusion.3
  131.5 0.4 fusion.1
  131.9 0.4 fusion
  132.3 0.9 fusion.2
  133.2 0.0 collective-permute-done.1
  133.2 1.6 %maximum_select_fusion = f32[64,9216]{1,0:T(8,128)} fusion(f32[32,9216]{1,0:T(8,128)S(1)} %collective-permute-done.1, f32[32,9216]{1,0:T(8,128)S(1)} %dynamic-slice_subtract_fusion, pred[]{:T(512)S(6)} %eq.4), kind=kLoop, calls=%fused_computation | loop fusion | flops 1769472 | bytes 4718593 | tf_op jit(solution)/shard_map/jit(_where)/select_n | solution.py:185
  (6 shorter events, 0.0 us)
Async XLA Ops:
  48.2 6.1 %copy-start.8 = (f32[1,2,64]{2,1,0:T(2,128)S(1)}, f32[1,2,64]{2,1,0:T(2,128)}, u32[]{:S(2)}) copy-start(f32[1,2,64]{2,1,0:T(2,128)} %param.10) | copy-start | bytes 1540
  48.2 7.7 %copy-start.7 = (f32[2,64]{1,0:T(2,128)S(1)}, f32[2,64]{1,0:T(2,128)}, u32[]{:S(2)}) copy-start(f32[2,64]{1,0:T(2,128)} %param.15) | copy-start | bytes 1540
  48.2 7.7 %copy-start.9 = (f32[2,64]{1,0:T(2,128)S(1)}, f32[2,64]{1,0:T(2,128)}, u32[]{:S(2)}) copy-start(f32[2,64]{1,0:T(2,128)} %param.16) | copy-start | bytes 1540
  48.3 7.7 %copy-start.10 = (f32[2,64]{1,0:T(2,128)S(1)}, f32[2,64]{1,0:T(2,128)}, u32[]{:S(2)}) copy-start(f32[2,64]{1,0:T(2,128)} %param.17) | copy-start | bytes 1540
  48.3 8.2 %copy-start.4 = (f32[576,256]{1,0:T(8,128)S(1)}, f32[576,256]{1,0:T(8,128)}, u32[]{:S(2)}) copy-start(f32[576,256]{1,0:T(8,128)} %param.13) | copy-start | bytes 1769476
  48.3 8.2 %copy-start.5 = (f32[576,256]{1,0:T(8,128)S(1)}, f32[576,256]{1,0:T(8,128)}, u32[]{:S(2)}) copy-start(f32[576,256]{1,0:T(8,128)} %param.14) | copy-start | bytes 1769476
  52.0 4.5 %collective-permute-start = (f32[576,256]{1,0:T(8,128)S(1)}, f32[576,256]{1,0:T(8,128)S(1)}, u32[]{:S(2)}, u32[]{:S(2)}) collective-permute-start(f32[576,256]{1,0:T(8,128)S(1)} %convolution_bitcast_fusion), channel_id=1, source_target_pairs={{0,16},{16,0},{1,17},{17,1},{2,18},{18,2},{3,19},{19,3},{4,20},{20... | collective-permute-start | bytes 1769480 | tf_op jit(solution)/shard_map/ppermute | solution.py:182
  54.3 1.6 %collective-permute-start.4 = (f32[2,64]{1,0:T(2,128)S(1)}, f32[2,64]{1,0:T(2,128)S(1)}, u32[]{:S(2)}, u32[]{:S(2)}) collective-permute-start(f32[2,64]{1,0:T(2,128)S(1)} %bitcast.34), channel_id=1, source_target_pairs={{0,16},{16,0},{1,17},{17,1},{2,18},{18,2},{3,19},{19,3},{4,20},{20... | collective-permute-start | bytes 1544 | tf_op jit(solution)/shard_map/ppermute | solution.py:182
  56.5 1.0 copy-start.6
  56.7 3.6 %copy-start = (f32[576,256]{1,0:T(8,128)}, f32[576,256]{1,0:T(8,128)S(1)}, u32[]{:S(2)}) copy-start(f32[576,256]{1,0:T(8,128)S(1)} %get-tuple-element.20) | copy-start | bytes 1769476
  56.7 3.6 %copy-start.1 = (f32[576,256]{1,0:T(8,128)}, f32[576,256]{1,0:T(8,128)S(1)}, u32[]{:S(2)}) copy-start(f32[576,256]{1,0:T(8,128)S(1)} %get-tuple-element.21) | copy-start | bytes 1769476
  57.5 2.8 %copy-start.2 = (f32[16,32,576]{2,1,0:T(8,128)S(1)}, f32[16,32,576]{2,1,0:T(8,128)}, u32[]{:S(2)}) copy-start(f32[16,32,576]{2,1,0:T(8,128)} %get-tuple-element.11) | copy-start | bytes 3538948
  120.7 4.7 %copy-start.3 = (f32[16,32,576]{2,1,0:T(8,128)S(1)}, f32[16,32,576]{2,1,0:T(8,128)}, u32[]{:S(2)}) copy-start(f32[16,32,576]{2,1,0:T(8,128)} %get-tuple-element.13) | copy-start | bytes 3538948
  123.1 5.7 %collective-permute-start.3 = (f32[256,256]{1,0:T(8,128)S(1)}, f32[256,256]{1,0:T(8,128)S(1)}, u32[]{:S(2)}, u32[]{:S(2)}) collective-permute-start(f32[256,256]{1,0:T(8,128)S(1)} %convolution_bitcast_fusion.1), channel_id=1, source_target_pairs={{0,16},{16,0},{1,17},{17,1},{2,18},{18,2},{3,19},{19,3},{4,20},{20... | collective-permute-start | bytes 786440 | tf_op jit(solution)/shard_map/ppermute | solution.py:182
  125.4 5.6 %collective-permute-start.2 = (f32[32,256]{1,0:T(8,128)S(1)}, f32[32,256]{1,0:T(8,128)S(1)}, u32[]{:S(2)}, u32[]{:S(2)}) collective-permute-start(f32[32,256]{1,0:T(8,128)S(1)} %dynamic-slice_bitcast_fusion), channel_id=1, source_target_pairs={{0,16},{16,0},{1,17},{17,1},{2,18},{18,2},{3,19},{19,3},{4,20},{20... | collective-permute-start | bytes 98312 | tf_op jit(solution)/shard_map/ppermute | solution.py:182
  128.2 5.0 %collective-permute-start.1 = (f32[32,9216]{1,0:T(8,128)S(1)}, f32[32,9216]{1,0:T(8,128)S(1)}, u32[]{:S(2)}, u32[]{:S(2)}) collective-permute-start(f32[32,9216]{1,0:T(8,128)S(1)} %dynamic-slice_subtract_fusion), channel_id=1, source_target_pairs={{0,16},{16,0},{1,17},{17,1},{2,18},{18,2},{3,19},{19,3},{4,20},{20... | collective-permute-start | bytes 3538952 | tf_op jit(solution)/shard_map/ppermute | solution.py:182

commit v3 on v2

--- a/solution.py
+++ b/solution.py
@@ -6,6 +6,7 @@
 from jax.sharding import PartitionSpec as P
 
 NS_STEPS = 3
+GRANT = 24 << 20
 
 
 beta_first = 0.9
@@ -41,27 +42,64 @@
     pl.semaphore_wait(barrier, len(others))
 
 
+def groups(n):
+    fan = 4 if n % 4 == 0 else 1
+    return n // fan, fan
+
+
+def peer_maps(n, me):
+    depth, fan = groups(n)
+    layer, spot = me // fan, lax.rem(me, fan)
+    column = {d: lax.rem(layer + d, depth) * fan + spot for d in range(1, depth)}
+    plane = {f: layer * fan + lax.rem(spot + f, fan) for f in range(1, fan)}
+    return layer, spot, column, plane
+
+
+def spread(n, me, ref, send, recv, sent):
+    depth, fan = groups(n)
+    layer, spot, column, plane = peer_maps(n, me)
+    down = []
+    for d in sorted(column, key=lambda d: abs(d - depth // 2)):
+        down.append((d, peer_copy(ref.at[me], ref.at[me], send.at[d * fan], recv.at[d * fan], {"grp": column[d]})))
+        down[-1][1].start()
+    for f in plane:
+        sent.append(peer_copy(ref.at[me], ref.at[me], send.at[f], recv.at[f], {"grp": plane[f]}))
+        sent[-1].start()
+
+    def pass_on():
+        for d, copy in down:
+            copy.wait()
+            slot = lax.rem(layer - d + depth, depth) * fan + spot
+            for f in plane:
+                at = d * fan + f
+                sent.append(peer_copy(ref.at[slot], ref.at[slot], send.at[at], recv.at[at], {"grp": plane[f]}))
+                sent[-1].start()
+
+    return pass_on
+
+
 def scatter_grad(n, grad, basis, cols, full, swap, parts, swap_sems, basis_send, basis_recv, col_send, col_recv):
     me, rep = lax.axis_index("grp"), lax.axis_index("rep")
     half = swap.shape[0]
     block = cols.shape[2]
     offsets = far_first(n)
     peers = {k: {"grp": lax.rem(me + k, n)} for k in offsets}
-    greet([{"rep": 1 - rep}] + [peers[k] for k in offsets])
     own = pl.ds(pl.multiple_of(rep * half, half), half)
     other = pl.ds(pl.multiple_of((1 - rep) * half, half), half)
+    full[pl.ds(me, 1)] = basis[own][None]
+    greet([{"rep": 1 - rep}] + [peers[k] for k in offsets])
     trade = peer_copy(grad.at[other], swap, swap_sems.at[0], swap_sems.at[1], {"rep": 1 - rep})
     trade.start()
     copies = []
-    for k in offsets:
-        copies.append(peer_copy(basis.at[own], full.at[me], basis_send.at[k], basis_recv.at[k], peers[k]))
-        copies[-1].start()
-    full[pl.ds(me, 1)] = basis[own][None]
+    pass_on = spread(n, me, full, basis_send, basis_recv, copies)
     trade.wait()
     for j in range(n):
         parts[j] = grad[own, j * block : (j + 1) * block] + swap[:, j * block : (j + 1) * block]
     cols[pl.ds(me, 1)] = parts[pl.ds(me, 1)]
-    for k in offsets:
+    late = n // 4
+    for at, k in enumerate(offsets):
+        if at == late:
+            pass_on()
         target = peers[k]["grp"]
         copies.append(peer_copy(parts.at[target], cols.at[me], col_send.at[k], col_recv.at[k], peers[k]))
         copies[-1].start()
@@ -69,39 +107,56 @@
         copy.wait()
 
 
-def reduce_and_return(n, terms, moved, rows, update, arrived, term_send, term_recv, row_send, row_recv, up_send, up_recv):
+def reduce_and_return(
+    n, terms, moved, rows, update, near, sums, far, near_send, near_recv, far_send, far_recv, row_send, row_recv, up_send, up_recv
+):
     me = lax.axis_index("grp")
+    depth, fan = groups(n)
+    layer, spot, column, plane = peer_maps(n, me)
     offsets = far_first(n)
     peers = {k: {"grp": lax.rem(me + k, n)} for k in offsets}
     greet([peers[k] for k in offsets])
-
-    def send_update(some):
-        for k in some:
+    late = []
+    waiting = list(offsets)
+
+    def send_update(count):
+        for k in waiting[:count]:
             copy = peer_copy(moved.at[peers[k]["grp"]], update.at[me], up_send.at[k], up_recv.at[k], peers[k])
             copy.start()
             late.append(copy)
-
-    late, early = [], []
-    for k in offsets:
-        copy = peer_copy(terms.at[peers[k]["grp"]], arrived.at[me], term_send.at[k], term_recv.at[k], peers[k])
-        copy.start()
-        early.append(copy)
-    first = n // 4
-    send_update(offsets[:first])
-    arrived[pl.ds(me, 1)] = terms[pl.ds(me, 1)]
+        del waiting[:count]
+
+    first = []
+    for f in plane:
+        source = terms.at[:, lax.rem(spot + f, fan)]
+        first.append(peer_copy(source, near.at[f], near_send.at[f], near_recv.at[f], {"grp": plane[f]}))
+        first[-1].start()
+    send_update(n // 4)
     update[pl.ds(me, 1)] = moved[pl.ds(me, 1)]
-    for copy in early:
+    near[0] = terms[:, pl.ds(spot, 1)][:, 0]
+    for copy in first:
         copy.wait()
-    total = arrived[0]
-    for j in range(1, n):
-        total = total + arrived[j]
+    partial = near[0]
+    for f in plane:
+        partial = partial + near[f]
+    sums[...] = partial
+    second = []
+    for d in column:
+        source = sums.at[lax.rem(layer + d, depth)]
+        second.append(peer_copy(source, far.at[d], far_send.at[d], far_recv.at[d], {"grp": column[d]}))
+        second[-1].start()
+    send_update(n // 8)
+    far[0] = sums[pl.ds(layer, 1)][0]
+    for copy in second:
+        copy.wait()
+    total = far[0]
+    for d in column:
+        total = total + far[d]
     rows[pl.ds(me, 1)] = total[None]
-    send_update(offsets[first : first + 2])
-    for k in offsets:
-        copy = peer_copy(rows.at[me], rows.at[me], row_send.at[k], row_recv.at[k], peers[k])
-        copy.start()
-        late.append(copy)
-    send_update(offsets[first + 2 :])
+    pass_on = spread(n, me, rows, row_send, row_recv, late)
+    send_update(n // 4)
+    pass_on()
+    send_update(n)
     for copy in late:
         copy.wait()
 
@@ -131,23 +186,30 @@
             sems,
             sems,
         ],
-        compiler_params=pltpu.CompilerParams(collective_id=0, has_side_effects=True),
+        compiler_params=pltpu.CompilerParams(collective_id=0, has_side_effects=True, vmem_limit_bytes=GRANT),
         name="scatter_grad",
     )(grad, basis)
 
 
 def call_return(n, terms, moved):
+    half, rank = terms.shape[2:]
+    depth, fan = groups(n)
     sems = pltpu.SemaphoreType.DMA((n,))
     return pl.pallas_call(
         lambda *refs: reduce_and_return(n, *refs),
         out_shape=(
-            jax.ShapeDtypeStruct(terms.shape, jnp.float32),
+            jax.ShapeDtypeStruct((n, half, rank), jnp.float32),
             jax.ShapeDtypeStruct(moved.shape, jnp.float32),
         ),
         in_specs=in_vmem(2),
         out_specs=tuple(in_vmem(2)),
-        scratch_shapes=[pltpu.VMEM(terms.shape, jnp.float32)] + [sems] * 6,
-        compiler_params=pltpu.CompilerParams(collective_id=1, has_side_effects=True),
+        scratch_shapes=[
+            pltpu.VMEM((fan, depth, half, rank), jnp.float32),
+            pltpu.VMEM((depth, half, rank), jnp.float32),
+            pltpu.VMEM((depth, half, rank), jnp.float32),
+        ]
+        + [sems] * 8,
+        compiler_params=pltpu.CompilerParams(collective_id=1, has_side_effects=True, vmem_limit_bytes=GRANT),
         name="reduce_and_return",
     )(terms, moved)
 
@@ -193,7 +255,7 @@
     new_first = beta_first * moment_first + (1.0 - beta_first) * projected
     new_second = beta_second * moment_second + (1.0 - beta_second) * projected * projected
     direction = new_first / corr_first / (jnp.sqrt(new_second / corr_second) + adam_eps)
-    terms = exact_dot(col_block, projected).reshape(n, half, rank)
+    terms = exact_dot(col_block, projected).reshape(*groups(n), half, rank)
     update_cols = exact_dot(half_basis, direction.T).reshape(n, half, block)
     sub_all, update = call_return(n, terms, update_cols)
     sub_half = lax.dynamic_index_in_dim(sub_all, lax.axis_index("grp"), 0, keepdims=False)

time: 136 us -> 108 us (0.79)
  Pallas kernels: 106 us -> 81.9 us
  matrix products: 13.9 us -> 9.28 us
    pallas_call x1, Pallas kernels: 58.2 us -> 42.9 us  [call_return(): pl.pallas_call(lambda *refs: reduce_and_return(n, *refs), out_shape=(jax....]
    pallas_call x1, Pallas kernels: 47.6 us -> 39.1 us  [call_scatter(): pl.pallas_call(lambda *refs: scatter_grad(n, *refs), out_shape=(jax.Shape...]
    dot_general x11, matrix products: 13.9 us -> 9.28 us  [exact_dot(): jnp.dot(left, right, precision=lax.Precision.HIGHEST, preferred_element_t...]
    unnamed x22 -> x16, local copies, waits for them, and re-layouts: 0.85 us -> 2.54 us
where the time goes in v3:
time: 108 us
  Pallas kernels  81.9 us (76%)
  matrix products  9.28 us (9%)
  other arithmetic  5.8 us (5%)
  starting transfers between devices  3.78 us (4%)
  local copies, waits for them, and re-layouts  3.77 us (3%)
  between operations  1.57 us (1%)
  waiting for transfers between devices  1.55 us (1%)
    pallas_call x1, Pallas kernels, call_return(): pl.pallas_call(lambda *refs: reduce_and_return(n, *refs), out_shape=(jax....  42.9 us
    pallas_call x1, Pallas kernels, call_scatter(): pl.pallas_call(lambda *refs: scatter_grad(n, *refs), out_shape=(jax.Shape...  39.1 us
    dot_general x11, matrix products, exact_dot(): jnp.dot(left, right, precision=lax.Precision.HIGHEST, preferred_element_t...  9.28 us
    ppermute x5, starting transfers between devices, swapped(): return lax.ppermute(x, 'rep', swap)  3.78 us
    unnamed x16, local copies, waits for them, and re-layouts  2.54 us
  transfers between devices with their start and end apart: 5, of which 1 were waited for; matrix products, arithmetic and copies ran while one was open for 6% of the time, Pallas kernels for 0%

profile of v3, /device:TPU:17, one launch (start us, length us, event | category | flops | bytes accessed | tf_op | source)
XLA Modules:
  0.0 107.7 jit_solution(6781838932284427781)
XLA Ops:
  0.6 0.0 copy-start
  0.6 1.7 %copy-done = f32[1,64,9216]{2,1,0:T(8,128)S(1)} copy-done((f32[1,64,9216]{2,1,0:T(8,128)S(1)}, f32[1,64,9216]{2,1,0:T(8,128)}, u32[]{:S(2)}) %copy-start) | copy-done | bytes 2359320
  2.3 0.0 copy-start.1
  2.3 0.8 copy-done.1
  3.1 39.1 %scatter_grad.1 = (f32[16,32,576]{2,1,0:T(8,128)S(1)}, f32[16,32,256]{2,1,0:T(8,128)S(1)}) custom-call(f32[64,9216]{1,0:T(8,128)S(1)} %bitcast.36, f32[64,256]{1,0:T(8,128)S(1)} %copy-done.1), custom_call_target="tpu_custom_call" | custom-call | tf_op jit(solution)/shard_map/scatter_grad/pallas_call | solution.py:172
  42.2 0.0 copy-start.5
  42.2 0.0 copy-start.4
  42.3 0.0 copy-start.6
  42.3 0.0 copy-start.7
  42.3 2.2 %convolution_bitcast_fusion = f32[576,256]{1,0:T(8,128)S(1)} fusion(f32[16,32,576]{2,1,0:T(8,128)S(1)} %get-tuple-element.11, f32[16,32,256]{2,1,0:T(8,128)S(1)} %get-tuple-element.12), kind=kOutput, calls=%fused_computation.2 | convolution fusion | flops 905969664 | bytes 2293760 | tf_op jit(solution)/shard_map/dot_general | solution.py:20
  44.5 1.1 %collective-permute-start = (f32[576,256]{1,0:T(8,128)S(1)}, f32[576,256]{1,0:T(8,128)S(1)}, u32[]{:S(2)}, u32[]{:S(2)}) collective-permute-start(f32[576,256]{1,0:T(8,128)S(1)} %convolution_bitcast_fusion), channel_id=1, source_target_pairs={{0,16},{16,0},{1,17},{17,1},{2,18},{18,2},{3,19},{19,3},{4,20},{20... | collective-permute-start | bytes 1769480 | tf_op jit(solution)/shard_map/ppermute | solution.py:244
  45.6 0.0 copy-done.5
  45.6 0.1 collective-permute-start.4
  45.7 1.5 %collective-permute-done.4 = f32[2,64]{1,0:T(2,128)S(1)} collective-permute-done((f32[2,64]{1,0:T(2,128)S(1)}, f32[2,64]{1,0:T(2,128)S(1)}, u32[]{:S(2)}, u32[]{:S(2)}) %collective-permute-start.4) | collective-permute-done | bytes 544 | tf_op jit(solution)/shard_map/ppermute | solution.py:244
  47.2 0.0 copy-done.4
  47.2 0.0 copy-done.6
  47.2 0.0 copy-done.7
  47.2 0.6 divide_subtract_fusion
  47.8 0.0 collective-permute-done
  47.8 1.4 %multiply_add_fusion = (f32[576,256]{1,0:T(8,128)S(1)}, f32[576,256]{1,0:T(8,128)S(1)}) fusion(f32[576,256]{1,0:T(8,128)} %param.13, f32[576,256]{1,0:T(8,128)S(1)} %convolution_bitcast_fusion, f32[576,256]{1,0:T(8,128)S(1)} %collective-permute-done, f32[576,256]{1,0:T(8,128)} %param.14), kind=kLoop, calls=%fused_computation.27 | loop fusion | flops 1179648 | bytes 3538944 | tf_op jit(solution)/shard_map/add | solution.py:255
  49.2 0.0 copy-start.2
  49.3 0.0 copy-start.3
  49.3 1.7 %fusion.7.refs_1_ = f32[16,32,576]{2,1,0:T(8,128)S(1)} fusion(f32[16,32,256]{2,1,0:T(8,128)S(1)} %get-tuple-element.12, f32[576,256]{1,0:T(8,128)S(1)} %get-tuple-element.21, f32[576,256]{1,0:T(8,128)S(1)} %get-tuple-element.20), kind=kOutput, calls=%fused_computation.20 | convolution fusion | flops 906559488 | bytes 2883584 | tf_op jit(solution)/shard_map/dot_general | solution.py:20
  51.0 0.0 copy-done.2
  51.0 0.0 copy-done.3
  51.0 1.4 %fusion.5.refs_0_ = f32[4,4,32,256]{3,2,1,0:T(8,128)S(1)} fusion(f32[4,4,32,576]{3,2,1,0:T(8,128)S(1)} %bitcast.37, f32[576,256]{1,0:T(8,128)S(1)} %convolution_bitcast_fusion, f32[576,256]{1,0:T(8,128)S(1)} %collective-permute-done), kind=kOutput, calls=%fused_computation.18 | convolution fusion | flops 906117120 | bytes 2883584 | tf_op jit(solution)/shard_map/dot_general | solution.py:20
  52.4 42.9 %reduce_and_return.1 = (f32[16,32,256]{2,1,0:T(8,128)S(1)}, f32[16,32,576]{2,1,0:T(8,128)S(1)}) custom-call(f32[4,4,32,256]{3,2,1,0:T(8,128)S(1)} %fusion.5.refs_0_, f32[16,32,576]{2,1,0:T(8,128)S(1)} %fusion.7.refs_1_), custom_call_target="tpu_custom_call" | custom-call | tf_op jit(solution)/shard_map/reduce_and_return/pallas_call | solution.py:198
  95.2 1.0 convolution_bitcast_fusion.1
  96.3 2.0 %collective-permute-start.3 = (f32[256,256]{1,0:T(8,128)S(1)}, f32[256,256]{1,0:T(8,128)S(1)}, u32[]{:S(2)}, u32[]{:S(2)}) collective-permute-start(f32[256,256]{1,0:T(8,128)S(1)} %convolution_bitcast_fusion.1), channel_id=1, source_target_pairs={{0,16},{16,0},{1,17},{17,1},{2,18},{18,2},{3,19},{19,3},{4,20},{20... | collective-permute-start | bytes 786440 | tf_op jit(solution)/shard_map/ppermute | solution.py:244
  98.3 0.1 collective-permute-start.2
  98.4 0.1 multiply_bitcast_fusion
  98.5 0.8 copy.16
  99.3 0.5 mul.129
  99.8 1.4 %dynamic-slice_subtract_fusion = f32[32,9216]{1,0:T(8,128)S(1)} fusion(f32[32,9216]{1,0:T(8,128)S(1)} %mul.129, f32[64,9216]{1,0:T(8,128)} %param.11, s32[]{:T(128)S(6)} %select_n.24), kind=kLoop, calls=%fused_computation.3 | loop fusion | flops 294912 | bytes 3538948 | tf_op jit(solution)/shard_map/sub | solution.py:267
  101.2 0.5 collective-permute-start.1
  101.7 0.0 collective-permute-done.3
  101.7 0.7 multiply_reduce_fusion
  103.1 0.4 convolution_multiply_fusion.3
  103.5 0.4 multiply_subtract_fusion
  103.9 0.0 collective-permute-done.2
  103.9 0.3 convolution_multiply_fusion.6
  104.2 0.3 fusion.3
  104.4 0.4 fusion.1
  104.8 0.4 fusion
  105.2 0.9 fusion.2
  106.1 0.0 collective-permute-done.1
  106.1 1.6 %maximum_select_fusion = f32[64,9216]{1,0:T(8,128)} fusion(f32[32,9216]{1,0:T(8,128)S(1)} %collective-permute-done.1, f32[32,9216]{1,0:T(8,128)S(1)} %dynamic-slice_subtract_fusion, pred[]{:T(512)S(6)} %eq.4), kind=kLoop, calls=%fused_computation | loop fusion | flops 1769472 | bytes 4718593 | tf_op jit(solution)/shard_map/jit(_where)/select_n | solution.py:247
  (1 shorter events, 0.0 us)
Async XLA Ops:
  0.6 1.7 %copy-start = (f32[1,64,9216]{2,1,0:T(8,128)S(1)}, f32[1,64,9216]{2,1,0:T(8,128)}, u32[]{:S(2)}) copy-start(f32[1,64,9216]{2,1,0:T(8,128)} %param.9) | copy-start | bytes 7077892
  2.3 0.8 copy-start.1
  42.2 3.3 %copy-start.5 = (f32[1,2,64]{2,1,0:T(2,128)S(1)}, f32[1,2,64]{2,1,0:T(2,128)}, u32[]{:S(2)}) copy-start(f32[1,2,64]{2,1,0:T(2,128)} %param.10) | copy-start | bytes 1540
  42.2 5.0 %copy-start.4 = (f32[2,64]{1,0:T(2,128)S(1)}, f32[2,64]{1,0:T(2,128)}, u32[]{:S(2)}) copy-start(f32[2,64]{1,0:T(2,128)} %param.15) | copy-start | bytes 1540
  42.3 5.0 %copy-start.6 = (f32[2,64]{1,0:T(2,128)S(1)}, f32[2,64]{1,0:T(2,128)}, u32[]{:S(2)}) copy-start(f32[2,64]{1,0:T(2,128)} %param.16) | copy-start | bytes 1540
  42.3 4.9 %copy-start.7 = (f32[2,64]{1,0:T(2,128)S(1)}, f32[2,64]{1,0:T(2,128)}, u32[]{:S(2)}) copy-start(f32[2,64]{1,0:T(2,128)} %param.17) | copy-start | bytes 1540
  44.5 3.3 %collective-permute-start = (f32[576,256]{1,0:T(8,128)S(1)}, f32[576,256]{1,0:T(8,128)S(1)}, u32[]{:S(2)}, u32[]{:S(2)}) collective-permute-start(f32[576,256]{1,0:T(8,128)S(1)} %convolution_bitcast_fusion), channel_id=1, source_target_pairs={{0,16},{16,0},{1,17},{17,1},{2,18},{18,2},{3,19},{19,3},{4,20},{20... | collective-permute-start | bytes 1769480 | tf_op jit(solution)/shard_map/ppermute | solution.py:244
  45.6 1.6 %collective-permute-start.4 = (f32[2,64]{1,0:T(2,128)S(1)}, f32[2,64]{1,0:T(2,128)S(1)}, u32[]{:S(2)}, u32[]{:S(2)}) collective-permute-start(f32[2,64]{1,0:T(2,128)S(1)} %bitcast.38), channel_id=1, source_target_pairs={{0,16},{16,0},{1,17},{17,1},{2,18},{18,2},{3,19},{19,3},{4,20},{20... | collective-permute-start | bytes 1544 | tf_op jit(solution)/shard_map/ppermute | solution.py:244
  49.2 1.7 %copy-start.2 = (f32[576,256]{1,0:T(8,128)}, f32[576,256]{1,0:T(8,128)S(1)}, u32[]{:S(2)}) copy-start(f32[576,256]{1,0:T(8,128)S(1)} %get-tuple-element.20) | copy-start | bytes 1769476
  49.3 1.7 %copy-start.3 = (f32[576,256]{1,0:T(8,128)}, f32[576,256]{1,0:T(8,128)S(1)}, u32[]{:S(2)}) copy-start(f32[576,256]{1,0:T(8,128)S(1)} %get-tuple-element.21) | copy-start | bytes 1769476
  96.3 5.4 %collective-permute-start.3 = (f32[256,256]{1,0:T(8,128)S(1)}, f32[256,256]{1,0:T(8,128)S(1)}, u32[]{:S(2)}, u32[]{:S(2)}) collective-permute-start(f32[256,256]{1,0:T(8,128)S(1)} %convolution_bitcast_fusion.1), channel_id=1, source_target_pairs={{0,16},{16,0},{1,17},{17,1},{2,18},{18,2},{3,19},{19,3},{4,20},{20... | collective-permute-start | bytes 786440 | tf_op jit(solution)/shard_map/ppermute | solution.py:244
  98.3 5.6 %collective-permute-start.2 = (f32[32,256]{1,0:T(8,128)S(1)}, f32[32,256]{1,0:T(8,128)S(1)}, u32[]{:S(2)}, u32[]{:S(2)}) collective-permute-start(f32[32,256]{1,0:T(8,128)S(1)} %dynamic-slice_bitcast_fusion), channel_id=1, source_target_pairs={{0,16},{16,0},{1,17},{17,1},{2,18},{18,2},{3,19},{19,3},{4,20},{20... | collective-permute-start | bytes 98312 | tf_op jit(solution)/shard_map/ppermute | solution.py:244
  101.2 4.9 %collective-permute-start.1 = (f32[32,9216]{1,0:T(8,128)S(1)}, f32[32,9216]{1,0:T(8,128)S(1)}, u32[]{:S(2)}, u32[]{:S(2)}) collective-permute-start(f32[32,9216]{1,0:T(8,128)S(1)} %dynamic-slice_subtract_fusion), channel_id=1, source_target_pairs={{0,16},{16,0},{1,17},{17,1},{2,18},{18,2},{3,19},{19,3},{4,20},{20... | collective-permute-start | bytes 3538952 | tf_op jit(solution)/shard_map/ppermute | solution.py:244

commit v4 on v3

--- a/solution.py
+++ b/solution.py
@@ -78,7 +78,50 @@
     return pass_on
 
 
-def scatter_grad(n, grad, basis, cols, full, swap, parts, swap_sems, basis_send, basis_recv, col_send, col_recv):
+def split_of(half, block):
+    rest = block % 128
+    return (block - rest, rest) if 2 * rest == 128 and half % 16 == 0 else (block, 0)
+
+
+def tails_of(n, half, block):
+    rest = split_of(half, block)[1]
+    return pltpu.VMEM((n, half // 2, 128) if rest else (1, 8, 128), jnp.float32)
+
+
+def pack_tails(ref, tails):
+    half = ref.shape[1]
+    main, rest = split_of(half, ref.shape[2])
+    if rest:
+        tails[:, :, :rest] = ref[:, : half // 2, main:]
+        tails[:, :, rest:] = ref[:, half // 2 :, main:]
+
+
+def unpack_tails(tails, ref):
+    half = ref.shape[1]
+    main, rest = split_of(half, ref.shape[2])
+    if rest:
+        ref[:, : half // 2, main:] = tails[:, :, :rest]
+        ref[:, half // 2 :, main:] = tails[:, :, rest:]
+
+
+def keep_own(me, source, target, tails_out, tails_in):
+    target[pl.ds(me, 1)] = source[pl.ds(me, 1)]
+    if split_of(*source.shape[1:])[1]:
+        tails_in[pl.ds(me, 1)] = tails_out[pl.ds(me, 1)]
+
+
+def send_block(me, k, where, source, target, tails_out, tails_in, send, recv):
+    main, rest = split_of(*source.shape[1:])
+    peer = where["grp"]
+    copies = [peer_copy(source.at[peer, :, :main], target.at[me, :, :main], send.at[0, k], recv.at[0, k], where)]
+    if rest:
+        copies.append(peer_copy(tails_out.at[peer], tails_in.at[me], send.at[1, k], recv.at[1, k], where))
+    for copy in copies:
+        copy.start()
+    return copies
+
+
+def scatter_grad(n, grad, basis, cols, full, mine, swap, parts, tails_out, tails_in, load_sem, swap_sems, basis_send, basis_recv, col_send, col_recv):
     me, rep = lax.axis_index("grp"), lax.axis_index("rep")
     half = swap.shape[0]
     block = cols.shape[2]
@@ -86,29 +129,32 @@
     peers = {k: {"grp": lax.rem(me + k, n)} for k in offsets}
     own = pl.ds(pl.multiple_of(rep * half, half), half)
     other = pl.ds(pl.multiple_of((1 - rep) * half, half), half)
+    load = pltpu.make_async_copy(grad.at[own], mine, load_sem)
+    load.start()
     full[pl.ds(me, 1)] = basis[own][None]
     greet([{"rep": 1 - rep}] + [peers[k] for k in offsets])
     trade = peer_copy(grad.at[other], swap, swap_sems.at[0], swap_sems.at[1], {"rep": 1 - rep})
     trade.start()
     copies = []
     pass_on = spread(n, me, full, basis_send, basis_recv, copies)
+    load.wait()
     trade.wait()
     for j in range(n):
-        parts[j] = grad[own, j * block : (j + 1) * block] + swap[:, j * block : (j + 1) * block]
-    cols[pl.ds(me, 1)] = parts[pl.ds(me, 1)]
+        parts[j] = mine[:, j * block : (j + 1) * block] + swap[:, j * block : (j + 1) * block]
+    pack_tails(parts, tails_out)
+    keep_own(me, parts, cols, tails_out, tails_in)
     late = n // 4
     for at, k in enumerate(offsets):
         if at == late:
             pass_on()
-        target = peers[k]["grp"]
-        copies.append(peer_copy(parts.at[target], cols.at[me], col_send.at[k], col_recv.at[k], peers[k]))
-        copies[-1].start()
+        copies += send_block(me, k, peers[k], parts, cols, tails_out, tails_in, col_send, col_recv)
     for copy in copies:
         copy.wait()
+    unpack_tails(tails_in, cols)
 
 
 def reduce_and_return(
-    n, terms, moved, rows, update, near, sums, far, near_send, near_recv, far_send, far_recv, row_send, row_recv, up_send, up_recv
+    n, terms, moved, rows, update, near, sums, far, tails_out, tails_in, near_send, near_recv, far_send, far_recv, row_send, row_recv, up_send, up_recv
 ):
     me = lax.axis_index("grp")
     depth, fan = groups(n)
@@ -121,9 +167,7 @@
 
     def send_update(count):
         for k in waiting[:count]:
-            copy = peer_copy(moved.at[peers[k]["grp"]], update.at[me], up_send.at[k], up_recv.at[k], peers[k])
-            copy.start()
-            late.append(copy)
+            late.extend(send_block(me, k, peers[k], moved, update, tails_out, tails_in, up_send, up_recv))
         del waiting[:count]
 
     first = []
@@ -131,8 +175,9 @@
         source = terms.at[:, lax.rem(spot + f, fan)]
         first.append(peer_copy(source, near.at[f], near_send.at[f], near_recv.at[f], {"grp": plane[f]}))
         first[-1].start()
+    pack_tails(moved, tails_out)
     send_update(n // 4)
-    update[pl.ds(me, 1)] = moved[pl.ds(me, 1)]
+    keep_own(me, moved, update, tails_out, tails_in)
     near[0] = terms[:, pl.ds(spot, 1)][:, 0]
     for copy in first:
         copy.wait()
@@ -159,6 +204,7 @@
     send_update(n)
     for copy in late:
         copy.wait()
+    unpack_tails(tails_in, update)
 
 
 def in_vmem(count):
@@ -175,16 +221,20 @@
             jax.ShapeDtypeStruct((n, half, block), jnp.float32),
             jax.ShapeDtypeStruct((n, half, rank), jnp.float32),
         ),
-        in_specs=in_vmem(2),
+        in_specs=[pl.BlockSpec(memory_space=pltpu.HBM)] + in_vmem(1),
         out_specs=tuple(in_vmem(2)),
         scratch_shapes=[
             pltpu.VMEM((half, ncol), jnp.float32),
+            pltpu.VMEM((half, ncol), jnp.float32),
             pltpu.VMEM((n, half, block), jnp.float32),
+            tails_of(n, half, block),
+            tails_of(n, half, block),
+            pltpu.SemaphoreType.DMA,
             pltpu.SemaphoreType.DMA((2,)),
             sems,
             sems,
-            sems,
-            sems,
+            pltpu.SemaphoreType.DMA((2, n)),
+            pltpu.SemaphoreType.DMA((2, n)),
         ],
         compiler_params=pltpu.CompilerParams(collective_id=0, has_side_effects=True, vmem_limit_bytes=GRANT),
         name="scatter_grad",
@@ -207,8 +257,11 @@
             pltpu.VMEM((fan, depth, half, rank), jnp.float32),
             pltpu.VMEM((depth, half, rank), jnp.float32),
             pltpu.VMEM((depth, half, rank), jnp.float32),
+            tails_of(*moved.shape),
+            tails_of(*moved.shape),
         ]
-        + [sems] * 8,
+        + [sems] * 6
+        + [pltpu.SemaphoreType.DMA((2, n))] * 2,
         compiler_params=pltpu.CompilerParams(collective_id=1, has_side_effects=True, vmem_limit_bytes=GRANT),
         name="reduce_and_return",
     )(terms, moved)

time: 108 us -> 103 us (0.954)
  Pallas kernels: 81.9 us -> 77.3 us
    pallas_call x1, Pallas kernels: 39.1 us -> 36.6 us  [call_scatter(): pl.pallas_call(lambda *refs: scatter_grad(n, *refs), out_shape=(jax.Shape...]
    pallas_call x1, Pallas kernels: 42.9 us -> 40.7 us  [call_return(): pl.pallas_call(lambda *refs: reduce_and_return(n, *refs), out_shape=(jax....]
  transfers between devices with their start and end apart: 5 -> 5, of which waited for: 1 -> 1; matrix products, arithmetic and copies ran while one was open for 6% -> 7% of each run, Pallas kernels for 0% -> 0%
where the time goes in v4:
time: 103 us
  Pallas kernels  77.3 us (75%)
  matrix products  9.27 us (9%)
  other arithmetic  5.8 us (6%)
  local copies, waits for them, and re-layouts  3.77 us (4%)
  starting transfers between devices  3.28 us (3%)
  between operations  1.57 us (2%)
  waiting for transfers between devices  1.55 us (2%)
    pallas_call x1, Pallas kernels, call_return(): pl.pallas_call(lambda *refs: reduce_and_return(n, *refs), out_shape=(jax....  40.7 us
    pallas_call x1, Pallas kernels, call_scatter(): pl.pallas_call(lambda *refs: scatter_grad(n, *refs), out_shape=(jax.Shape...  36.6 us
    dot_general x11, matrix products, exact_dot(): jnp.dot(left, right, precision=lax.Precision.HIGHEST, preferred_element_t...  9.27 us
    ppermute x5, starting transfers between devices, swapped(): return lax.ppermute(x, 'rep', swap)  3.28 us
    unnamed x16, local copies, waits for them, and re-layouts  2.54 us
  transfers between devices with their start and end apart: 5, of which 1 were waited for; matrix products, arithmetic and copies ran while one was open for 7% of the time, Pallas kernels for 0%

profile of v4, /device:TPU:17, one launch (start us, length us, event | category | flops | bytes accessed | tf_op | source)
XLA Modules:
  0.0 102.5 jit_solution(11461720775831796460)
XLA Ops:
  0.6 0.0 copy-start
  0.6 1.7 %copy-done = f32[1,64,9216]{2,1,0:T(8,128)S(1)} copy-done((f32[1,64,9216]{2,1,0:T(8,128)S(1)}, f32[1,64,9216]{2,1,0:T(8,128)}, u32[]{:S(2)}) %copy-start) | copy-done | bytes 2359320
  2.3 0.0 copy-start.1
  2.3 0.8 copy-done.1
  3.1 36.6 %scatter_grad.1 = (f32[16,32,576]{2,1,0:T(8,128)S(1)}, f32[16,32,256]{2,1,0:T(8,128)S(1)}) custom-call(f32[64,9216]{1,0:T(8,128)S(1)} %bitcast.36, f32[64,256]{1,0:T(8,128)S(1)} %copy-done.1), custom_call_target="tpu_custom_call" | custom-call | tf_op jit(solution)/shard_map/scatter_grad/pallas_call | solution.py:218
  39.8 0.0 copy-start.5
  39.8 0.0 copy-start.4
  39.8 0.0 copy-start.6
  39.8 0.0 copy-start.7
  39.8 2.2 %convolution_bitcast_fusion = f32[576,256]{1,0:T(8,128)S(1)} fusion(f32[16,32,576]{2,1,0:T(8,128)S(1)} %get-tuple-element.11, f32[16,32,256]{2,1,0:T(8,128)S(1)} %get-tuple-element.12), kind=kOutput, calls=%fused_computation.2 | convolution fusion | flops 905969664 | bytes 2293760 | tf_op jit(solution)/shard_map/dot_general | solution.py:20
  42.0 1.1 %collective-permute-start = (f32[576,256]{1,0:T(8,128)S(1)}, f32[576,256]{1,0:T(8,128)S(1)}, u32[]{:S(2)}, u32[]{:S(2)}) collective-permute-start(f32[576,256]{1,0:T(8,128)S(1)} %convolution_bitcast_fusion), channel_id=1, source_target_pairs={{0,16},{16,0},{1,17},{17,1},{2,18},{18,2},{3,19},{19,3},{4,20},{20... | collective-permute-start | bytes 1769480 | tf_op jit(solution)/shard_map/ppermute | solution.py:297
  43.1 0.0 copy-done.5
  43.1 0.1 collective-permute-start.4
  43.2 1.5 %collective-permute-done.4 = f32[2,64]{1,0:T(2,128)S(1)} collective-permute-done((f32[2,64]{1,0:T(2,128)S(1)}, f32[2,64]{1,0:T(2,128)S(1)}, u32[]{:S(2)}, u32[]{:S(2)}) %collective-permute-start.4) | collective-permute-done | bytes 544 | tf_op jit(solution)/shard_map/ppermute | solution.py:297
  44.7 0.0 copy-done.4
  44.7 0.0 copy-done.6
  44.7 0.0 copy-done.7
  44.7 0.6 divide_subtract_fusion
  45.3 0.0 collective-permute-done
  45.3 1.4 %multiply_add_fusion = (f32[576,256]{1,0:T(8,128)S(1)}, f32[576,256]{1,0:T(8,128)S(1)}) fusion(f32[576,256]{1,0:T(8,128)} %param.13, f32[576,256]{1,0:T(8,128)S(1)} %convolution_bitcast_fusion, f32[576,256]{1,0:T(8,128)S(1)} %collective-permute-done, f32[576,256]{1,0:T(8,128)} %param.14), kind=kLoop, calls=%fused_computation.27 | loop fusion | flops 1179648 | bytes 3538944 | tf_op jit(solution)/shard_map/add | solution.py:308
  46.8 0.0 copy-start.2
  46.8 0.0 copy-start.3
  46.8 1.7 %fusion.7.refs_1_ = f32[16,32,576]{2,1,0:T(8,128)S(1)} fusion(f32[16,32,256]{2,1,0:T(8,128)S(1)} %get-tuple-element.12, f32[576,256]{1,0:T(8,128)S(1)} %get-tuple-element.21, f32[576,256]{1,0:T(8,128)S(1)} %get-tuple-element.20), kind=kOutput, calls=%fused_computation.20 | convolution fusion | flops 906559488 | bytes 2883584 | tf_op jit(solution)/shard_map/dot_general | solution.py:20
  48.5 0.0 copy-done.2
  48.5 0.0 copy-done.3
  48.5 1.4 %fusion.5.refs_0_ = f32[4,4,32,256]{3,2,1,0:T(8,128)S(1)} fusion(f32[4,4,32,576]{3,2,1,0:T(8,128)S(1)} %bitcast.37, f32[576,256]{1,0:T(8,128)S(1)} %convolution_bitcast_fusion, f32[576,256]{1,0:T(8,128)S(1)} %collective-permute-done), kind=kOutput, calls=%fused_computation.18 | convolution fusion | flops 906117120 | bytes 2883584 | tf_op jit(solution)/shard_map/dot_general | solution.py:20
  49.9 40.7 %reduce_and_return.1 = (f32[16,32,256]{2,1,0:T(8,128)S(1)}, f32[16,32,576]{2,1,0:T(8,128)S(1)}) custom-call(f32[4,4,32,256]{3,2,1,0:T(8,128)S(1)} %fusion.5.refs_0_, f32[16,32,576]{2,1,0:T(8,128)S(1)} %fusion.7.refs_1_), custom_call_target="tpu_custom_call" | custom-call | tf_op jit(solution)/shard_map/reduce_and_return/pallas_call | solution.py:248
  90.6 1.0 convolution_bitcast_fusion.1
  91.6 1.5 %collective-permute-start.3 = (f32[256,256]{1,0:T(8,128)S(1)}, f32[256,256]{1,0:T(8,128)S(1)}, u32[]{:S(2)}, u32[]{:S(2)}) collective-permute-start(f32[256,256]{1,0:T(8,128)S(1)} %convolution_bitcast_fusion.1), channel_id=1, source_target_pairs={{0,16},{16,0},{1,17},{17,1},{2,18},{18,2},{3,19},{19,3},{4,20},{20... | collective-permute-start | bytes 786440 | tf_op jit(solution)/shard_map/ppermute | solution.py:297
  93.2 0.1 collective-permute-start.2
  93.3 0.1 multiply_bitcast_fusion
  93.4 0.8 copy.16
  94.2 0.5 mul.129
  94.6 1.4 %dynamic-slice_subtract_fusion = f32[32,9216]{1,0:T(8,128)S(1)} fusion(f32[32,9216]{1,0:T(8,128)S(1)} %mul.129, f32[64,9216]{1,0:T(8,128)} %param.11, s32[]{:T(128)S(6)} %select_n.24), kind=kLoop, calls=%fused_computation.3 | loop fusion | flops 294912 | bytes 3538948 | tf_op jit(solution)/shard_map/sub | solution.py:320
  96.0 0.5 collective-permute-start.1
  96.5 0.0 collective-permute-done.3
  96.5 0.7 multiply_reduce_fusion
  97.9 0.4 convolution_multiply_fusion.3
  98.3 0.4 multiply_subtract_fusion
  98.7 0.0 collective-permute-done.2
  98.8 0.3 convolution_multiply_fusion.6
  99.0 0.3 fusion.3
  99.3 0.4 fusion.1
  99.7 0.4 fusion
  100.1 0.9 fusion.2
  100.9 0.0 collective-permute-done.1
  101.0 1.6 %maximum_select_fusion = f32[64,9216]{1,0:T(8,128)} fusion(f32[32,9216]{1,0:T(8,128)S(1)} %collective-permute-done.1, f32[32,9216]{1,0:T(8,128)S(1)} %dynamic-slice_subtract_fusion, pred[]{:T(512)S(6)} %eq.4), kind=kLoop, calls=%fused_computation | loop fusion | flops 1769472 | bytes 4718593 | tf_op jit(solution)/shard_map/jit(_where)/select_n | solution.py:300
  (1 shorter events, 0.0 us)
Async XLA Ops:
  0.6 1.7 %copy-start = (f32[1,64,9216]{2,1,0:T(8,128)S(1)}, f32[1,64,9216]{2,1,0:T(8,128)}, u32[]{:S(2)}) copy-start(f32[1,64,9216]{2,1,0:T(8,128)} %param.9) | copy-start | bytes 7077892
  2.3 0.8 copy-start.1
  39.8 3.3 %copy-start.5 = (f32[1,2,64]{2,1,0:T(2,128)S(1)}, f32[1,2,64]{2,1,0:T(2,128)}, u32[]{:S(2)}) copy-start(f32[1,2,64]{2,1,0:T(2,128)} %param.10) | copy-start | bytes 1540
  39.8 5.0 %copy-start.4 = (f32[2,64]{1,0:T(2,128)S(1)}, f32[2,64]{1,0:T(2,128)}, u32[]{:S(2)}) copy-start(f32[2,64]{1,0:T(2,128)} %param.15) | copy-start | bytes 1540
  39.8 5.0 %copy-start.6 = (f32[2,64]{1,0:T(2,128)S(1)}, f32[2,64]{1,0:T(2,128)}, u32[]{:S(2)}) copy-start(f32[2,64]{1,0:T(2,128)} %param.16) | copy-start | bytes 1540
  39.8 4.9 %copy-start.7 = (f32[2,64]{1,0:T(2,128)S(1)}, f32[2,64]{1,0:T(2,128)}, u32[]{:S(2)}) copy-start(f32[2,64]{1,0:T(2,128)} %param.17) | copy-start | bytes 1540
  42.0 3.3 %collective-permute-start = (f32[576,256]{1,0:T(8,128)S(1)}, f32[576,256]{1,0:T(8,128)S(1)}, u32[]{:S(2)}, u32[]{:S(2)}) collective-permute-start(f32[576,256]{1,0:T(8,128)S(1)} %convolution_bitcast_fusion), channel_id=1, source_target_pairs={{0,16},{16,0},{1,17},{17,1},{2,18},{18,2},{3,19},{19,3},{4,20},{20... | collective-permute-start | bytes 1769480 | tf_op jit(solution)/shard_map/ppermute | solution.py:297
  43.1 1.6 %collective-permute-start.4 = (f32[2,64]{1,0:T(2,128)S(1)}, f32[2,64]{1,0:T(2,128)S(1)}, u32[]{:S(2)}, u32[]{:S(2)}) collective-permute-start(f32[2,64]{1,0:T(2,128)S(1)} %bitcast.38), channel_id=1, source_target_pairs={{0,16},{16,0},{1,17},{17,1},{2,18},{18,2},{3,19},{19,3},{4,20},{20... | collective-permute-start | bytes 1544 | tf_op jit(solution)/shard_map/ppermute | solution.py:297
  46.8 1.7 %copy-start.2 = (f32[576,256]{1,0:T(8,128)}, f32[576,256]{1,0:T(8,128)S(1)}, u32[]{:S(2)}) copy-start(f32[576,256]{1,0:T(8,128)S(1)} %get-tuple-element.20) | copy-start | bytes 1769476
  46.8 1.7 %copy-start.3 = (f32[576,256]{1,0:T(8,128)}, f32[576,256]{1,0:T(8,128)S(1)}, u32[]{:S(2)}) copy-start(f32[576,256]{1,0:T(8,128)S(1)} %get-tuple-element.21) | copy-start | bytes 1769476
  91.6 4.9 %collective-permute-start.3 = (f32[256,256]{1,0:T(8,128)S(1)}, f32[256,256]{1,0:T(8,128)S(1)}, u32[]{:S(2)}, u32[]{:S(2)}) collective-permute-start(f32[256,256]{1,0:T(8,128)S(1)} %convolution_bitcast_fusion.1), channel_id=1, source_target_pairs={{0,16},{16,0},{1,17},{17,1},{2,18},{18,2},{3,19},{19,3},{4,20},{20... | collective-permute-start | bytes 786440 | tf_op jit(solution)/shard_map/ppermute | solution.py:297
  93.2 5.6 %collective-permute-start.2 = (f32[32,256]{1,0:T(8,128)S(1)}, f32[32,256]{1,0:T(8,128)S(1)}, u32[]{:S(2)}, u32[]{:S(2)}) collective-permute-start(f32[32,256]{1,0:T(8,128)S(1)} %dynamic-slice_bitcast_fusion), channel_id=1, source_target_pairs={{0,16},{16,0},{1,17},{17,1},{2,18},{18,2},{3,19},{19,3},{4,20},{20... | collective-permute-start | bytes 98312 | tf_op jit(solution)/shard_map/ppermute | solution.py:297
  96.0 4.9 %collective-permute-start.1 = (f32[32,9216]{1,0:T(8,128)S(1)}, f32[32,9216]{1,0:T(8,128)S(1)}, u32[]{:S(2)}, u32[]{:S(2)}) collective-permute-start(f32[32,9216]{1,0:T(8,128)S(1)} %dynamic-slice_subtract_fusion), channel_id=1, source_target_pairs={{0,16},{16,0},{1,17},{17,1},{2,18},{18,2},{3,19},{19,3},{4,20},{20... | collective-permute-start | bytes 3538952 | tf_op jit(solution)/shard_map/ppermute | solution.py:297
